TPU v7x, 1024 devices: a whole 4x8x16 slice. The times are simulated.
1024 devices in a mesh: context: 16 (over z), head: 64 (over y, x, core).
Axes of the slice: x: 4, y: 8, z: 16, core: 2. Of those that a mesh axis runs over, the one named last changes fastest.
Arguments:
- x_in: bfloat16 [16384, 16384], P('context', 'head'), may hold values from -6 to 6
- bc_in: bfloat16 [16384, 4096], P('context'), may hold values from -6 to 6
- z_in: bfloat16 [16384, 16384], P('context', 'head'), may hold values from -6 to 6
- dt_in: bfloat16 [256, 16384], P('head', 'context'), may hold values from -4 to 4
- conv_x_w: float32 [4, 16384], P(None, 'head'), may hold values from -3 to 3
- conv_x_b: float32 [16384], P('head'), may hold values from -1.5 to 1.5
- conv_bc_w: float32 [4, 4096], replicated, may hold values from -3 to 3
- conv_bc_b: float32 [4096], replicated, may hold values from -1.5 to 1.5
- dt_bias: float32 [256], P('head'), may hold values from -3.5 to -2.5
- a_log: float32 [256], P('head'), may hold values from -12 to 0
- skip_gain: float32 [256], P('head'), may hold values from 1 to 4
- norm_w: float32 [16384], P('head'), may hold values from 0.5 to 1.5
- doc_len: int32 [64], replicated, may hold values from 1 to 8192, 16384 in all
Outputs:
- ssd_out: bfloat16 [16384, 16384], P('context', 'head')
Inputs may be any that keep to these rules, and one draw needn't show every extreme that they name: `doc_len`: the lengths sum to 16384; the longest is exactly 8192.
All inputs are finite; a program needn't handle non-finite values.
Results may differ from a plain program's by a relative error of at most 0.0034.
Values may be sent and summed in bfloat16 or wider, within the bound.
No kernel may reach another device: no remote copies, remote signals or barrier semaphores. Data moves between devices by JAX's collectives and lax.ppermute only.
A program may use at most 64 MiB of HBM per device.

v0:
```python
import jax
import jax.numpy as jnp
from jax import lax
from jax.sharding import PartitionSpec as P

HEAD_DIM = 64
STATE = 256
GROUPS = 8
CONV = 4
BLOCK = 256


exact_mode = lax.Precision.HIGHEST
norm_floor = 1e-05


def from_behind(shard, axis, by):
    count = lax.axis_size(axis)
    pairs = [(i, i + by) for i in range(count) if 0 <= i + by < count]
    return lax.ppermute(shard, axis, pairs)


def entering_2(part, axis, combine, identity):
    place = lax.axis_index(axis)
    gathered = jax.tree.map(lambda a: lax.all_gather(a, axis), part)
    state = jax.tree.map(lambda a, e: jnp.zeros_like(a) + jnp.asarray(e, a.dtype), part, identity)

    def one(hop, state):
        return combine(
            state, jax.tree.map(lambda a: lax.dynamic_index_in_dim(a, hop, 0, False), gathered)
        )

    return lax.fori_loop(0, place, one, state)


def sent_to_all(shard, axis):
    copies = jnp.broadcast_to(shard, (lax.axis_size(axis), *shard.shape))
    return lax.all_to_all(copies, axis, split_axis=0, concat_axis=0, tiled=True)


def taken_together(shard, axis):
    everything = sent_to_all(shard, axis)
    return jnp.sum(everything, axis=0)


def doc_marks(doc_len, positions):
    doc_ends = jnp.cumsum(doc_len)
    begins = doc_ends - doc_len
    segment = jnp.sum((doc_ends[None, :] <= positions[:, None]).astype(jnp.int32), axis=1)
    opening = jnp.sum((begins[None, :] == positions[:, None]).astype(jnp.int32), axis=1)
    return (segment, opening)


def conv_silu(extended, segment_ext, weights, biases, rows_count):
    newest = segment_ext[CONV - 1 : CONV - 1 + rows_count]
    summed = jnp.zeros((rows_count, extended.shape[1]), jnp.float32) + biases[None, :]
    for offset in range(CONV):
        same_doc = (segment_ext[offset : offset + rows_count] == newest).astype(jnp.float32)
        summed = (
            summed
            + weights[offset][None, :]
            * extended[offset : offset + rows_count].astype(jnp.float32)
            * same_doc[:, None]
        )
    return jax.nn.silu(summed).astype(jnp.bfloat16)


def combine_states(first_part, second_part):
    return (
        first_part[0] * second_part[0],
        second_part[0][:, None, None] * first_part[1] + second_part[1],
    )


def shards(
    x_in,
    bc_in,
    z_in,
    dt_in,
    conv_x_w,
    conv_x_b,
    conv_bc_w,
    conv_bc_b,
    dt_bias,
    a_log,
    skip_gain,
    norm_w,
    doc_len,
):
    rows_here = x_in.shape[0]
    heads_here = dt_in.shape[0]
    width_here = x_in.shape[1]
    heads_total = heads_here * lax.axis_size("head")
    per_group = heads_total // GROUPS
    group_index = lax.axis_index("head") * heads_here // per_group
    b_raw = lax.dynamic_slice_in_dim(bc_in, group_index * STATE, STATE, 1)
    c_raw = lax.dynamic_slice_in_dim(bc_in, (GROUPS + group_index) * STATE, STATE, 1)
    raw_rows = jnp.concatenate([x_in, b_raw, c_raw], axis=1)
    weights = jnp.concatenate(
        [
            conv_x_w,
            lax.dynamic_slice_in_dim(conv_bc_w, group_index * STATE, STATE, 1),
            lax.dynamic_slice_in_dim(conv_bc_w, (GROUPS + group_index) * STATE, STATE, 1),
        ],
        axis=1,
    )
    biases = jnp.concatenate(
        [
            conv_x_b,
            lax.dynamic_slice_in_dim(conv_bc_b, group_index * STATE, STATE, 0),
            lax.dynamic_slice_in_dim(conv_bc_b, (GROUPS + group_index) * STATE, STATE, 0),
        ],
        axis=0,
    )
    before = from_behind(raw_rows[rows_here - (CONV - 1) :], "context", 1)
    extended = jnp.concatenate([before, raw_rows], axis=0)
    first_pos = lax.axis_index("context") * rows_here
    positions_ext = first_pos - (CONV - 1) + jnp.arange(rows_here + CONV - 1, dtype=jnp.int32)
    segment_ext, opening_ext = doc_marks(doc_len, positions_ext)
    mixed = conv_silu(extended, segment_ext, weights, biases, rows_here)
    segment = segment_ext[CONV - 1 :]
    opening = opening_ext[CONV - 1 :]
    blocks = rows_here // BLOCK
    x_vals = mixed[:, :width_here].astype(jnp.float32).reshape(blocks, BLOCK, heads_here, HEAD_DIM)
    b_vals = (
        mixed[:, width_here : width_here + STATE].astype(jnp.float32).reshape(blocks, BLOCK, STATE)
    )
    c_vals = mixed[:, width_here + STATE :].astype(jnp.float32).reshape(blocks, BLOCK, STATE)
    step_size = jax.nn.softplus(dt_in.astype(jnp.float32) + dt_bias[:, None])
    log_decay = (step_size * (-jnp.exp(a_log))[:, None]).reshape(heads_here, blocks, BLOCK)
    running = jnp.cumsum(log_decay, axis=2)
    step_blocks = jnp.transpose(step_size.reshape(heads_here, blocks, BLOCK), (1, 2, 0))
    weighted = x_vals * step_blocks[..., None]
    seg_blocks = segment.reshape(blocks, BLOCK)
    alive_mask = jnp.cumsum(opening.reshape(blocks, BLOCK), axis=1) == 0
    lower_tri = jnp.arange(BLOCK)[:, None] >= jnp.arange(BLOCK)[None, :]
    same_block = (seg_blocks[:, :, None] == seg_blocks[:, None, :]) & lower_tri[None]
    inner_prod = jnp.einsum("ctn,csn->cts", c_vals, b_vals, precision=exact_mode)
    gap_logs = jnp.minimum(running[:, :, :, None] - running[:, :, None, :], 0.0)
    mixing = jnp.where(same_block[None], jnp.exp(gap_logs), 0.0) * inner_prod[None]
    intra_out = jnp.einsum("hcts,cshp->cthp", mixing, weighted, precision=exact_mode)
    tail_weight = jnp.where(
        (seg_blocks == seg_blocks[:, -1:])[None], jnp.exp(running[:, :, -1:] - running), 0.0
    )
    tail_blocks = jnp.transpose(tail_weight, (1, 2, 0))
    summaries = jnp.einsum(
        "cshp,csn->chpn", weighted * tail_blocks[..., None], b_vals, precision=exact_mode
    )
    carry_decay = jnp.transpose(
        jnp.exp(running[:, :, -1]) * alive_mask[None, :, -1].astype(jnp.float32)
    )

    def advance(carry_now, inputs):
        state_now, decay_now = carry_now
        summary, factor = inputs
        return (
            (factor[:, None, None] * state_now + summary, decay_now * factor),
            (state_now, decay_now),
        )

    zero_state = jnp.zeros((heads_here, HEAD_DIM, STATE), jnp.float32)
    unit_decay = jnp.ones((heads_here,), jnp.float32)
    (local_end, local_decay), (local_in, decay_in) = lax.scan(
        advance, (zero_state, unit_decay), (summaries, carry_decay)
    )
    prefix = entering_2(
        (local_decay, local_end), "context", combine_states, (unit_decay, zero_state)
    )
    entering = prefix[1]
    incoming = local_in + decay_in[:, :, None, None] * entering[None]
    entry_scale = jnp.transpose(alive_mask[None].astype(jnp.float32) * jnp.exp(running), (1, 2, 0))
    from_state = (
        jnp.einsum("ctn,chpn->cthp", c_vals, incoming, precision=exact_mode)
        * entry_scale[..., None]
    )
    outputs = intra_out + from_state + skip_gain[None, None, :, None] * x_vals
    outputs = outputs.reshape(rows_here, width_here)
    gated_out = outputs * jax.nn.silu(z_in.astype(jnp.float32))
    squares = jnp.sum(gated_out * gated_out, axis=1)
    total_squares = taken_together(squares, "head")
    mean_square = total_squares / (heads_total * HEAD_DIM)
    result = gated_out * lax.rsqrt(mean_square + norm_floor)[:, None] * norm_w[None, :]
    return result.astype(jnp.bfloat16)


def solution(mesh):
    return jax.shard_map(
        shards,
        mesh=mesh,
        in_specs=(
            P("context", "head"),
            P("context", None),
            P("context", "head"),
            P("head", "context"),
            P(None, "head"),
            P("head"),
            P(),
            P(),
            P("head"),
            P("head"),
            P("head"),
            P("head"),
            P(),
        ),
        out_specs=P("context", "head"),
        check_vma=False,
    )
```

profile of v0, /device:TPU:1, one launch (start us, length us, event | category | flops | bytes accessed | tf_op | source)
XLA Modules:
  0.0 159.5 jit_solution(17672925519342315248)
XLA Ops:
  6.6 1.3 constant_dynamic-slice_fusion.2
  8.0 1.1 pad_maximum_fusion
  9.1 4.8 %collective-permute-start = (bf16[3,768]{1,0:T(4,128)(2,1)S(1)}, bf16[3,768]{1,0:T(4,128)(2,1)S(1)}, u32[]{:S(2)}, u32[]{:S(2)}) collective-permute-start(bf16[3,768]{1,0:T(4,128)(2,1)S(1)} %slice.96), channel_id=1, source_target_pairs={{0,64},{64,128},{128,192},{192,256},{256,320},{320,384},{384,448},... | collective-permute-start | bytes 13832 | tf_op jit(solution)/shard_map/ppermute | solution.py:20
  14.6 0.7 constant_dynamic-slice_fusion.4
  15.4 0.8 fusion.38
  16.2 1.2 reduce-window.31
  18.0 4.8 %reduce-window.24 = f32[4,4,2,128]{3,2,1,0:T(2,128)S(1)} reduce-window(f32[4,4,2,128]{3,2,1,0:T(2,128)S(1)} %reshape.184, f32[]{:T(128)} %constant.95.clone.1), window={size=1x1x1x128 pad=0_0x0_0x0_0x127_0}, to_apply=%region_2.3 | reduce-window | flops 520192 | bytes 32772 | tf_op jit(solution)/shard_map/reduce-window.1
  24.6 3.0 %multiply_convert_fusion = bf16[1024,768]{1,0:T(8,128)(2,1)S(1)} fusion(bf16[1027,768]{1,0:T(8,128)(2,1)S(1)} %maximum_maximum_fusion, f32[768]{0:T(1024)S(1)} %get-tuple-element.161, f32[1024]{0:T(1024)S(1)} %get-tuple-element.211, f32[768]{0:T(1024)S(1)} %get-tuple-element.162, f32[1024]{0:T(1024)S(1)} %get-tuple-element.212, ...), kind=kLoop, calls=%fused_computation.15 | loop fusion | flops 19660800 | bytes 7891968 | tf_op jit(solution)/shard_map/convert_element_type | solution.py:65
  28.6 1.3 broadcast_multiply_fusion
  29.8 0.7 fusion.23
  30.6 3.6 %while.30 = (s32[]{:T(128)}, f32[4,64,256]{2,1,0:T(8,128)S(1)}, f32[4]{0:T(128)S(1)}, f32[4,4,64,256]{3,2,1,0:T(8,128)}, f32[4,4]{1,0:T(4,128)S(1)}, /*index=5*/...) while((s32[]{:T(128)}, f32[4,64,256]{2,1,0:T(8,128)S(1)}, ...), condition=%wide.region_8.9_spmd.clone, body=%wide.region_7.8_spmd.clone.sunk | while | flops 262155 | bytes 1310977 | solution.py:163
  30.6 0.7 bitcast_dynamic-update-slice_fusion.2
  31.5 0.7 bitcast_dynamic-update-slice_fusion.2
  32.4 0.7 bitcast_dynamic-update-slice_fusion.2
  33.3 0.7 bitcast_dynamic-update-slice_fusion.2
  34.2 0.7 copy-done
  34.9 1.2 copy.114
  36.1 1.3 dynamic-slice
  38.6 33.9 %all-reduce = f32[64]{0:T(128)S(1)} all-reduce(f32[64]{0:T(128)S(1)} %dynamic-update-slice), channel_id=2, replica_groups=mesh['context'=16,'head'=64] {'context'}, use_global_device_ids=true, to_apply=%add | all-reduce | flops 64 | bytes 512
  73.0 7.1 %fusion.16 = f32[4,256,4,64]{1,3,2,0:T(8,128)} fusion(f32[4,256,256]{2,1,0:T(8,128)S(1)} %fusion.39, f32[4,4,256]{2,0,1:T(4,128)S(1)} %get-tuple-element.207, pred[4,256,256]{2,1,0:T(8,128)(4,1)S(1)} %compare_and_fusion, f32[4,256,4,64]{1,0,3,2:T(4,128)} %get-tuple-element.195), kind=kOutput, calls=%fused_computation.26 | convolution fusion | flops 809500672 | bytes 3424256 | tf_op jit(solution)/shard_map/hcts,cshp->cthp/dot_general | solution.py:141
  80.1 34.9 %all-gather.4.cloned.1.call-done = f32[64,64,256]{2,1,0:T(8,128)} async-done(((f32[4,64,256]{2,1,0:T(8,128)}), f32[64,64,256]{2,1,0:T(8,128)}) %all-gather.4.cloned.1.call-update) | async-done | bytes 4194320 | tf_op jit(solution)/shard_map/all_gather | solution.py:25
  115.2 2.5 %fusion.15 = f32[4,256,4,64]{1,3,2,0:T(8,128)S(1)} fusion(f32[4,256,4,64]{1,3,2,0:T(8,128)} %fusion.16, bf16[4,256,256,1]{2,1,3,0:T(8,128)(2,1)S(1)} %bitcast.69, f32[4,256,4,64]{1,0,3,2:T(4,128)S(1)} %reshape.192, f32[4,4,64,256]{3,2,1,0:T(8,128)} %get-tuple-element.89, f32[4]{0:T(128)S(1)} %copy-done.8, f32[4,256,4]{1,2,0:T(4,128)S(1)} %get-tuple-element.206, ...), kind=kOutput, calls=%fused_computation.25 | convolution fusion | flops 806879232 | bytes 4997200 | tf_op jit(solution)/shard_map/ctn,chpn->cthp/dot_general | solution.py:173
  119.1 31.9 %all_to_all.6 = f32[64,1,1024]{2,1,0:T(1,128)S(1)} all-to-all(f32[64,1,1024]{2,1,0:T(1,128)S(1)} %broadcast_in_dim.40), channel_id=1, replica_groups=mesh['context'=16,'head'=64] {'head'}, dimensions={0} | all-to-all | bytes 524288 | tf_op jit(solution)/shard_map/all_to_all | solution.py:38
  151.7 1.0 copy.116
  (98 shorter events, 7.7 us)
Async XLA Ops:
  6.5 17.7 %copy-start.1 = (bf16[1024,256]{1,0:T(8,128)(2,1)S(1)}, bf16[1024,256]{1,0:T(8,128)(2,1)}, u32[]{:S(2)}) copy-start(bf16[1024,256]{1,0:T(8,128)(2,1)} %param.17) | copy-start | bytes 1572868
  6.5 7.4 %copy-start.6 = (s32[64]{0:T(128)S(1)}, s32[64]{0:T(128)}, u32[]{:S(2)}) copy-start(s32[64]{0:T(128)} %param.29) | copy-start | bytes 772
  6.5 8.8 %copy-start.3 = (f32[4,256]{1,0:T(4,128)S(1)}, f32[4,256]{1,0:T(4,128)}, u32[]{:S(2)}) copy-start(f32[4,256]{1,0:T(4,128)} %param.21) | copy-start | bytes 12292
  6.5 11.3 %copy-start.9 = (f32[4]{0:T(128)S(1)}, f32[4]{0:T(128)}, u32[]{:S(2)}) copy-start(f32[4]{0:T(128)} %param.26) | copy-start | bytes 52
  6.5 11.3 %copy-start.7 = (f32[4]{0:T(128)S(1)}, f32[4]{0:T(128)}, u32[]{:S(2)}) copy-start(f32[4]{0:T(128)} %param.25) | copy-start | bytes 52
  6.5 11.3 %copy-start.2 = (bf16[4,1024]{1,0:T(4,128)(2,1)S(1)}, bf16[4,1024]{1,0:T(4,128)(2,1)}, u32[]{:S(2)}) copy-start(bf16[4,1024]{1,0:T(4,128)(2,1)} %param.20) | copy-start | bytes 24580
  6.6 17.5 %copy-start.5 = (f32[256]{0:T(256)S(1)}, f32[256]{0:T(256)}, u32[]{:S(2)}) copy-start(f32[256]{0:T(256)} %param.22) | copy-start | bytes 3076
  6.6 108.4 %all-gather.4.cloned.1.call-start = ((), (), s32[]{:S(2)}) async-start(), calls=%async_computation.1 | async-start | bytes 4456448 | tf_op jit(solution)/shard_map/all_gather | solution.py:25
  9.1 15.1 %collective-permute-start = (bf16[3,768]{1,0:T(4,128)(2,1)S(1)}, bf16[3,768]{1,0:T(4,128)(2,1)S(1)}, u32[]{:S(2)}, u32[]{:S(2)}) collective-permute-start(bf16[3,768]{1,0:T(4,128)(2,1)S(1)} %slice.96), channel_id=1, source_target_pairs={{0,64},{64,128},{128,192},{192,256},{256,320},{320,384},{384,448},... | collective-permute-start | bytes 13832 | tf_op jit(solution)/shard_map/ppermute | solution.py:20
  34.1 0.7 copy-start
  80.1 35.1 %copy-start.8 = (f32[4]{0:T(128)S(1)}, f32[4]{0:T(128)}, u32[]{:S(2)}) copy-start(f32[4]{0:T(128)} %param.27) | copy-start | bytes 52
  117.7 33.6 %copy-start.4 = (f32[256]{0:T(256)S(1)}, f32[256]{0:T(256)}, u32[]{:S(2)}) copy-start(f32[256]{0:T(256)} %param.28) | copy-start | bytes 3076
Sparse Core Ops, SparseCore 0:
  35.0 79.9 all-gather.3
where the time goes:
time: 162 us; the launch traced here: 159 us
  blocking collectives  65.9 us (41%)
  waiting for transfers between devices  34.9 us (22%)
  other arithmetic  17.6 us (11%)
  between operations  14.5 us (9%)
  local copies, waits for them, and re-layouts  10.9 us (7%)
  matrix products  10.6 us (7%)
  starting transfers between devices  4.85 us (3%)
    all_gather x1, waiting for transfers between devices, entering_2(): gathered = jax.tree.map(lambda a: lax.all_gather(a, axis), part)  34.9 us
    unnamed x1, blocking collectives  33.9 us
    all_to_all x1, blocking collectives, sent_to_all(): return lax.all_to_all(copies, axis, split_axis=0, concat_axis=0, tiled=True)  31.9 us
    dot_general x1, matrix products, shards(): jnp.einsum('hcts,cshp->cthp', mixing, weighted, precision=exact_mode)  7.13 us
    another operation x8, other arithmetic  6.38 us
    ppermute x1, starting transfers between devices, from_behind(): return lax.ppermute(shard, axis, pairs)  4.81 us
    unnamed x27, local copies, waits for them, and re-layouts  3.93 us
  transfers between devices with their start and end apart: 2, of which 1 were waited for; matrix products, arithmetic and copies ran while one was open for 13% of the time, Pallas kernels for 0%

commit v1 on v0

--- a/solution.py
+++ b/solution.py
@@ -10,7 +10,6 @@
 BLOCK = 256
 
 
-exact_mode = lax.Precision.HIGHEST
 norm_floor = 1e-05
 
 
@@ -20,27 +19,42 @@
     return lax.ppermute(shard, axis, pairs)
 
 
-def entering_2(part, axis, combine, identity):
-    place = lax.axis_index(axis)
-    gathered = jax.tree.map(lambda a: lax.all_gather(a, axis), part)
-    state = jax.tree.map(lambda a, e: jnp.zeros_like(a) + jnp.asarray(e, a.dtype), part, identity)
-
-    def one(hop, state):
-        return combine(
-            state, jax.tree.map(lambda a: lax.dynamic_index_in_dim(a, hop, 0, False), gathered)
-        )
-
-    return lax.fori_loop(0, place, one, state)
-
-
-def sent_to_all(shard, axis):
-    copies = jnp.broadcast_to(shard, (lax.axis_size(axis), *shard.shape))
-    return lax.all_to_all(copies, axis, split_axis=0, concat_axis=0, tiled=True)
+def split_pair(value):
+    high = value.astype(jnp.bfloat16)
+    return high, (value - high.astype(jnp.float32)).astype(jnp.bfloat16)
+
+
+def entering_state(decay, end):
+    count = lax.axis_size("context")
+    heads, dim, state = end.shape
+    width = heads * dim // count
+    slices = end.astype(jnp.bfloat16).reshape(count, width // 2, 2 * state)
+    high, rest = split_pair(decay)
+    middle, low = split_pair(decay - high.astype(jnp.float32))
+    parts = jnp.repeat(jnp.stack([high, middle, low], axis=1), count // heads, axis=0)
+    parts = jnp.pad(parts, ((0, 0), (0, 125)))
+    extra = jnp.broadcast_to(parts[:, None, :], (count, width // 2, 128))
+    sent = jnp.concatenate([slices, extra], axis=2)
+    got = lax.all_to_all(sent, "context", split_axis=0, concat_axis=0, tiled=True)
+    got = got.astype(jnp.float32)
+    factors = jnp.sum(got[:, 0, 2 * state : 2 * state + 3], axis=1)
+    ends = got[:, :, : 2 * state]
+    now = jnp.zeros_like(ends[0])
+    entering = []
+    for shard in range(count):
+        entering.append(now)
+        now = factors[shard] * now + ends[shard]
+    back = jnp.stack(entering).astype(jnp.bfloat16)
+    mine = lax.all_to_all(back, "context", split_axis=0, concat_axis=0, tiled=True)
+    return mine.reshape(heads, dim, state)
 
 
 def taken_together(shard, axis):
-    everything = sent_to_all(shard, axis)
-    return jnp.sum(everything, axis=0)
+    count = lax.axis_size(axis)
+    tile = shard.astype(jnp.bfloat16).reshape(1, -1, 128)
+    copies = jnp.broadcast_to(tile, (count, *tile.shape[1:]))
+    everything = lax.all_to_all(copies, axis, split_axis=0, concat_axis=0, tiled=True)
+    return jnp.sum(everything.astype(jnp.float32), axis=0).reshape(shard.shape)
 
 
 def doc_marks(doc_len, positions):
@@ -65,11 +79,8 @@
     return jax.nn.silu(summed).astype(jnp.bfloat16)
 
 
-def combine_states(first_part, second_part):
-    return (
-        first_part[0] * second_part[0],
-        second_part[0][:, None, None] * first_part[1] + second_part[1],
-    )
+def product(spec, left, right):
+    return jnp.einsum(spec, left, right, preferred_element_type=jnp.float32)
 
 
 def shards(
@@ -122,10 +133,8 @@
     opening = opening_ext[CONV - 1 :]
     blocks = rows_here // BLOCK
     x_vals = mixed[:, :width_here].astype(jnp.float32).reshape(blocks, BLOCK, heads_here, HEAD_DIM)
-    b_vals = (
-        mixed[:, width_here : width_here + STATE].astype(jnp.float32).reshape(blocks, BLOCK, STATE)
-    )
-    c_vals = mixed[:, width_here + STATE :].astype(jnp.float32).reshape(blocks, BLOCK, STATE)
+    b_vals = mixed[:, width_here : width_here + STATE].reshape(blocks, BLOCK, STATE)
+    c_vals = mixed[:, width_here + STATE :].reshape(blocks, BLOCK, STATE)
     step_size = jax.nn.softplus(dt_in.astype(jnp.float32) + dt_bias[:, None])
     log_decay = (step_size * (-jnp.exp(a_log))[:, None]).reshape(heads_here, blocks, BLOCK)
     running = jnp.cumsum(log_decay, axis=2)
@@ -135,44 +144,38 @@
     alive_mask = jnp.cumsum(opening.reshape(blocks, BLOCK), axis=1) == 0
     lower_tri = jnp.arange(BLOCK)[:, None] >= jnp.arange(BLOCK)[None, :]
     same_block = (seg_blocks[:, :, None] == seg_blocks[:, None, :]) & lower_tri[None]
-    inner_prod = jnp.einsum("ctn,csn->cts", c_vals, b_vals, precision=exact_mode)
+    inner_prod = product("ctn,csn->cts", c_vals, b_vals)
     gap_logs = jnp.minimum(running[:, :, :, None] - running[:, :, None, :], 0.0)
     mixing = jnp.where(same_block[None], jnp.exp(gap_logs), 0.0) * inner_prod[None]
-    intra_out = jnp.einsum("hcts,cshp->cthp", mixing, weighted, precision=exact_mode)
+    step_here = step_size.reshape(heads_here, blocks, 1, BLOCK)
+    mixing = (mixing * step_here).astype(jnp.bfloat16)
+    x_low = mixed[:, :width_here].reshape(blocks, BLOCK, heads_here, HEAD_DIM)
+    intra_out = product("hcts,cshp->cthp", mixing, x_low)
     tail_weight = jnp.where(
         (seg_blocks == seg_blocks[:, -1:])[None], jnp.exp(running[:, :, -1:] - running), 0.0
     )
     tail_blocks = jnp.transpose(tail_weight, (1, 2, 0))
-    summaries = jnp.einsum(
-        "cshp,csn->chpn", weighted * tail_blocks[..., None], b_vals, precision=exact_mode
-    )
+    high, low = split_pair(weighted * tail_blocks[..., None])
+    summaries = product("cshp,csn->chpn", high, b_vals) + product("cshp,csn->chpn", low, b_vals)
     carry_decay = jnp.transpose(
         jnp.exp(running[:, :, -1]) * alive_mask[None, :, -1].astype(jnp.float32)
     )
 
-    def advance(carry_now, inputs):
-        state_now, decay_now = carry_now
-        summary, factor = inputs
-        return (
-            (factor[:, None, None] * state_now + summary, decay_now * factor),
-            (state_now, decay_now),
-        )
-
-    zero_state = jnp.zeros((heads_here, HEAD_DIM, STATE), jnp.float32)
-    unit_decay = jnp.ones((heads_here,), jnp.float32)
-    (local_end, local_decay), (local_in, decay_in) = lax.scan(
-        advance, (zero_state, unit_decay), (summaries, carry_decay)
-    )
-    prefix = entering_2(
-        (local_decay, local_end), "context", combine_states, (unit_decay, zero_state)
-    )
-    entering = prefix[1]
-    incoming = local_in + decay_in[:, :, None, None] * entering[None]
+    state_now = jnp.zeros((heads_here, HEAD_DIM, STATE), jnp.float32)
+    decay_now = jnp.ones((heads_here,), jnp.float32)
+    local_in, decay_in = [], []
+    for block in range(blocks):
+        local_in.append(state_now)
+        decay_in.append(decay_now)
+        state_now = carry_decay[block][:, None, None] * state_now + summaries[block]
+        decay_now = decay_now * carry_decay[block]
+    local_in = jnp.stack(local_in).astype(jnp.bfloat16)
+    decay_in = jnp.stack(decay_in)
+    entering = entering_state(decay_now, state_now)
     entry_scale = jnp.transpose(alive_mask[None].astype(jnp.float32) * jnp.exp(running), (1, 2, 0))
-    from_state = (
-        jnp.einsum("ctn,chpn->cthp", c_vals, incoming, precision=exact_mode)
-        * entry_scale[..., None]
-    )
+    from_state = product("ctn,chpn->cthp", c_vals, local_in)
+    from_before = product("ctn,hpn->cthp", c_vals, entering) * decay_in[:, None, :, None]
+    from_state = (from_state + from_before) * entry_scale[..., None]
     outputs = intra_out + from_state + skip_gain[None, None, :, None] * x_vals
     outputs = outputs.reshape(rows_here, width_here)
     gated_out = outputs * jax.nn.silu(z_in.astype(jnp.float32))

time: 162 us -> 146 us (0.901)
  blocking collectives: 65.9 us -> 24.7 us
  other arithmetic: 17.6 us -> 49.8 us
  starting transfers between devices: 4.85 us -> 30.1 us
  waiting for transfers between devices: 34.9 us -> 16.7 us
  between operations: 14.5 us -> 1.29 us
  matrix products: 10.6 us -> 5.05 us
  local copies, waits for them, and re-layouts: 10.9 us -> 15.9 us
    all_gather x1 -> x0, waiting for transfers between devices: 34.9 us -> none  [entering_2(): gathered = jax.tree.map(lambda a: lax.all_gather(a, axis), part)]
    unnamed x1 -> x0, blocking collectives: 33.9 us -> none
    unnamed x3 -> x15, other arithmetic: 0.08 us -> 29.2 us
    all_to_all x0 -> x2, starting transfers between devices: none -> 25.3 us  [the longest x1 17.7 us: entering_state(): lax.all_to_all(sent, 'context', split_axis=0, concat_axis=0, tiled=True)]
    all_to_all x0 -> x2, waiting for transfers between devices: none -> 16.7 us  [the longest x1 8.41 us: entering_state(): lax.all_to_all(sent, 'context', split_axis=0, concat_axis=0, tiled=True)]
    all_to_all x1, blocking collectives: 31.9 us -> 24.7 us  [taken_together(): lax.all_to_all(copies, axis, split_axis=0, concat_axis=0, tiled=True)]
    dot_general x4 -> x6, matrix products: 10.6 us -> 5.05 us  [product(): return jnp.einsum(spec, left, right, preferred_element_type=jnp.float32)]
    another operation x8 -> x11, other arithmetic: 6.38 us -> 9.94 us
  transfers between devices with their start and end apart: 2 -> 3, of which waited for: 1 -> 2; matrix products, arithmetic and copies ran while one was open for 13% -> 15% of each run, Pallas kernels for 0% -> 0%
where the time goes in v1:
time: 146 us; the launch traced here: 143 us
  other arithmetic  49.8 us (34%)
  starting transfers between devices  30.1 us (21%)
  blocking collectives  24.7 us (17%)
  waiting for transfers between devices  16.7 us (11%)
  local copies, waits for them, and re-layouts  15.9 us (11%)
  matrix products  5.05 us (3%)
    unnamed x15, other arithmetic  29.2 us
    all_to_all x1, blocking collectives, taken_together(): lax.all_to_all(copies, axis, split_axis=0, concat_axis=0, tiled=True)  24.7 us
    all_to_all x1, starting transfers between devices, entering_state(): lax.all_to_all(sent, 'context', split_axis=0, concat_axis=0, tiled=True)  17.7 us
    all_to_all x1, waiting for transfers between devices, entering_state(): lax.all_to_all(sent, 'context', split_axis=0, concat_axis=0, tiled=True)  8.41 us
    all_to_all x1, waiting for transfers between devices, entering_state(): lax.all_to_all(back, 'context', split_axis=0, concat_axis=0, tiled=True)  8.25 us
    all_to_all x1, starting transfers between devices, entering_state(): lax.all_to_all(back, 'context', split_axis=0, concat_axis=0, tiled=True)  7.58 us
    another operation x8, other arithmetic  7.23 us
    dot_general x6, matrix products, product(): return jnp.einsum(spec, left, right, preferred_element_type=jnp.float32)  5.05 us
  transfers between devices with their start and end apart: 3, of which 2 were waited for; matrix products, arithmetic and copies ran while one was open for 15% of the time, Pallas kernels for 0%

profile of v1, /device:TPU:1, one launch (start us, length us, event | category | flops | bytes accessed | tf_op | source)
XLA Modules:
  0.0 143.5 jit_solution(3515479673170806788)
XLA Ops:
  0.1 1.3 constant_dynamic-slice_fusion.1
  2.6 4.8 %collective-permute-start = (bf16[3,768]{1,0:T(4,128)(2,1)S(1)}, bf16[3,768]{1,0:T(4,128)(2,1)S(1)}, u32[]{:S(2)}, u32[]{:S(2)}) collective-permute-start(bf16[3,768]{1,0:T(4,128)(2,1)S(1)} %slice.273), channel_id=1, source_target_pairs={{0,64},{64,128},{128,192},{192,256},{256,320},{320,384},{384,448},... | collective-permute-start | bytes 13832 | tf_op jit(solution)/shard_map/ppermute | solution.py:19
  8.2 4.8 %reduce-window.24 = f32[4,4,2,128]{3,2,1,0:T(2,128)S(1)} reduce-window(f32[4,4,2,128]{3,2,1,0:T(2,128)S(1)} %reshape.306, f32[]{:T(128)} %constant.71.clone.1), window={size=1x1x1x128 pad=0_0x0_0x0_0x127_0}, to_apply=%region_2.3 | reduce-window | flops 520192 | bytes 32772 | tf_op jit(solution)/shard_map/reduce-window.1
  22.2 3.0 %multiply_convert_fusion.1 = bf16[1024,768]{1,0:T(8,128)(2,1)S(1)} fusion(bf16[1027,768]{1,0:T(8,128)(2,1)S(1)} %maximum_maximum_fusion, f32[768]{0:T(1024)S(1)} %get-tuple-element.6, f32[1024]{0:T(1024)S(1)} %get-tuple-element.56, f32[768]{0:T(1024)S(1)} %get-tuple-element.7, f32[1024]{0:T(1024)S(1)} %get-tuple-element.57, f32[768]{0:T(1024)S(1)} %get-tuple-element.8, ...), kind=kLoop, calls=%fused_computation.1 | loop fusion | flops 19660800 | bytes 7891968 | tf_op jit(solution)/shard_map/convert_element_type | solution.py:79
  27.8 1.7 %squeeze.39 = f32[16,8,512]{2,1,0:T(8,128)} reshape(f32[1,4,64,256]{3,2,1,0:T(8,128)} %get-tuple-element.45) | data formatting | bytes 524288 | tf_op jit(solution)/shard_map/squeeze | solution.py:170
  33.1 17.7 %all-to-all-start = ((bf16[16,8,640]{2,1,0:T(8,128)(2,1)}), bf16[16,8,640]{2,1,0:T(8,128)(2,1)S(1)}, u32[]{:S(2)}, u32[]{:S(2)}) async-start(bf16[16,8,640]{2,1,0:T(8,128)(2,1)} %pad_maximum_fusion.1), calls=%async_computation | async-start | bytes 327680 | tf_op jit(solution)/shard_map/all_to_all | solution.py:38
  54.5 8.4 %all-to-all-done = bf16[16,8,640]{2,1,0:T(8,128)(2,1)S(1)} async-done(((bf16[16,8,640]{2,1,0:T(8,128)(2,1)}), bf16[16,8,640]{2,1,0:T(8,128)(2,1)S(1)}, u32[]{:S(2)}, u32[]{:S(2)}) %all-to-all-start) | async-done | bytes 163872 | tf_op jit(solution)/shard_map/all_to_all | solution.py:38
  66.4 1.9 %constant_dynamic-update-slice_fusion.12 = bf16[16,8,512]{2,1,0:T(8,128)(2,1)} fusion(bf16[16,8,512]{2,1,0:T(8,128)(2,1)} %get-tuple-element.30, f32[16,8,640]{2,1,0:T(8,128)} %copy-done.1, f32[1,8,512]{2,1,0:T(8,128)S(1)} %get-tuple-element.31, f32[]{:T(128)} %bitcast.23), kind=kLoop, calls=%fused_computation.66 | loop fusion | flops 12288 | bytes 41472
  68.2 2.5 %constant_dynamic-update-slice_fusion.11 = (bf16[16,8,512]{2,1,0:T(8,128)(2,1)}, f32[1,8,512]{2,1,0:T(8,128)S(1)}) fusion(bf16[16,8,512]{2,1,0:T(8,128)(2,1)} %constant_dynamic-update-slice_fusion.12, f32[16,8,640]{2,1,0:T(8,128)} %copy-done.1, f32[1,8,512]{2,1,0:T(8,128)S(1)} %get-tuple-element.31, f32[]{:T(128)} %bitcast.23, f32[]{:T(128)} %bitcast.24), kind=kLoop, calls=%fused_computation.65 | loop fusion | flops 20480 | bytes 74752
  70.8 1.9 %constant_dynamic-update-slice_fusion.10 = bf16[16,8,512]{2,1,0:T(8,128)(2,1)} fusion(bf16[16,8,512]{2,1,0:T(8,128)(2,1)} %get-tuple-element.28, f32[16,8,640]{2,1,0:T(8,128)} %copy-done.1, f32[1,8,512]{2,1,0:T(8,128)S(1)} %get-tuple-element.29, f32[]{:T(128)} %bitcast.25), kind=kLoop, calls=%fused_computation.64 | loop fusion | flops 12288 | bytes 41472
  72.7 2.6 %constant_dynamic-update-slice_fusion.9 = (bf16[16,8,512]{2,1,0:T(8,128)(2,1)}, f32[1,8,512]{2,1,0:T(8,128)S(1)}) fusion(bf16[16,8,512]{2,1,0:T(8,128)(2,1)} %constant_dynamic-update-slice_fusion.10, f32[16,8,640]{2,1,0:T(8,128)} %copy-done.1, f32[1,8,512]{2,1,0:T(8,128)S(1)} %get-tuple-element.29, f32[]{:T(128)} %bitcast.25, f32[]{:T(128)} %bitcast.26), kind=kLoop, calls=%fused_computation.63 | loop fusion | flops 20480 | bytes 74752
  75.3 2.0 %constant_dynamic-update-slice_fusion.8 = bf16[16,8,512]{2,1,0:T(8,128)(2,1)} fusion(bf16[16,8,512]{2,1,0:T(8,128)(2,1)} %get-tuple-element.26, f32[16,8,640]{2,1,0:T(8,128)} %copy-done.1, f32[1,8,512]{2,1,0:T(8,128)S(1)} %get-tuple-element.27, f32[]{:T(128)} %bitcast.27), kind=kLoop, calls=%fused_computation.62 | loop fusion | flops 12288 | bytes 41472
  77.2 2.6 %constant_dynamic-update-slice_fusion.7 = (bf16[16,8,512]{2,1,0:T(8,128)(2,1)}, f32[1,8,512]{2,1,0:T(8,128)S(1)}) fusion(bf16[16,8,512]{2,1,0:T(8,128)(2,1)} %constant_dynamic-update-slice_fusion.8, f32[16,8,640]{2,1,0:T(8,128)} %copy-done.1, f32[1,8,512]{2,1,0:T(8,128)S(1)} %get-tuple-element.27, f32[]{:T(128)} %bitcast.27, f32[]{:T(128)} %bitcast.28), kind=kLoop, calls=%fused_computation.61 | loop fusion | flops 20480 | bytes 74752
  79.8 1.9 %constant_dynamic-update-slice_fusion.6 = bf16[16,8,512]{2,1,0:T(8,128)(2,1)} fusion(bf16[16,8,512]{2,1,0:T(8,128)(2,1)} %get-tuple-element.24, f32[16,8,640]{2,1,0:T(8,128)} %copy-done.1, f32[1,8,512]{2,1,0:T(8,128)S(1)} %get-tuple-element.25, f32[]{:T(128)} %bitcast.29), kind=kLoop, calls=%fused_computation.60 | loop fusion | flops 12288 | bytes 41472
  81.8 2.7 %constant_dynamic-update-slice_fusion.5 = (bf16[16,8,512]{2,1,0:T(8,128)(2,1)}, f32[1,8,512]{2,1,0:T(8,128)S(1)}) fusion(bf16[16,8,512]{2,1,0:T(8,128)(2,1)} %constant_dynamic-update-slice_fusion.6, f32[16,8,640]{2,1,0:T(8,128)} %copy-done.1, f32[1,8,512]{2,1,0:T(8,128)S(1)} %get-tuple-element.25, f32[]{:T(128)} %bitcast.29, f32[]{:T(128)} %bitcast.30), kind=kLoop, calls=%fused_computation.59 | loop fusion | flops 20480 | bytes 74752
  84.4 2.0 %constant_dynamic-update-slice_fusion.4 = bf16[16,8,512]{2,1,0:T(8,128)(2,1)} fusion(bf16[16,8,512]{2,1,0:T(8,128)(2,1)} %get-tuple-element.22, f32[16,8,640]{2,1,0:T(8,128)} %copy-done.1, f32[1,8,512]{2,1,0:T(8,128)S(1)} %get-tuple-element.23, f32[]{:T(128)} %bitcast.31), kind=kLoop, calls=%fused_computation.58 | loop fusion | flops 12288 | bytes 41472
  86.4 2.6 %constant_dynamic-update-slice_fusion.3 = (bf16[16,8,512]{2,1,0:T(8,128)(2,1)}, f32[1,8,512]{2,1,0:T(8,128)S(1)}) fusion(bf16[16,8,512]{2,1,0:T(8,128)(2,1)} %constant_dynamic-update-slice_fusion.4, f32[16,8,640]{2,1,0:T(8,128)} %copy-done.1, f32[1,8,512]{2,1,0:T(8,128)S(1)} %get-tuple-element.23, f32[]{:T(128)} %bitcast.31, f32[]{:T(128)} %bitcast.32), kind=kLoop, calls=%fused_computation.57 | loop fusion | flops 20480 | bytes 74752
  89.0 2.0 %constant_dynamic-update-slice_fusion.2 = bf16[16,8,512]{2,1,0:T(8,128)(2,1)} fusion(bf16[16,8,512]{2,1,0:T(8,128)(2,1)} %get-tuple-element.20, f32[16,8,640]{2,1,0:T(8,128)} %copy-done.1, f32[1,8,512]{2,1,0:T(8,128)S(1)} %get-tuple-element.21, f32[]{:T(128)} %bitcast.33), kind=kLoop, calls=%fused_computation.56 | loop fusion | flops 12288 | bytes 41472
  91.0 2.6 %constant_dynamic-update-slice_fusion.1 = (bf16[16,8,512]{2,1,0:T(8,128)(2,1)}, f32[1,8,512]{2,1,0:T(8,128)S(1)}) fusion(bf16[16,8,512]{2,1,0:T(8,128)(2,1)} %constant_dynamic-update-slice_fusion.2, f32[16,8,640]{2,1,0:T(8,128)} %copy-done.1, f32[1,8,512]{2,1,0:T(8,128)S(1)} %get-tuple-element.21, f32[]{:T(128)} %bitcast.33, f32[]{:T(128)} %bitcast.34), kind=kLoop, calls=%fused_computation.55 | loop fusion | flops 20480 | bytes 74752
  93.7 1.9 %constant_dynamic-update-slice_fusion = bf16[16,8,512]{2,1,0:T(8,128)(2,1)} fusion(bf16[16,8,512]{2,1,0:T(8,128)(2,1)} %get-tuple-element.18, f32[16,8,640]{2,1,0:T(8,128)} %copy-done.1, f32[1,8,512]{2,1,0:T(8,128)S(1)} %get-tuple-element.19, f32[]{:T(128)} %bitcast.35), kind=kLoop, calls=%fused_computation.54 | loop fusion | flops 12288 | bytes 41472 | tf_op jit(solution)/shard_map/stack | solution.py:47
  95.6 7.6 %all-to-all-start.1 = ((bf16[16,8,512]{2,1,0:T(8,128)(2,1)}), bf16[16,8,512]{2,1,0:T(8,128)(2,1)S(1)}, u32[]{:S(2)}, u32[]{:S(2)}) async-start(bf16[16,8,512]{2,1,0:T(8,128)(2,1)} %constant_dynamic-update-slice_fusion), calls=%async_computation.1 | async-start | bytes 262144 | tf_op jit(solution)/shard_map/all_to_all | solution.py:48
  103.6 3.3 %fusion.7 = f32[4,256,4,64]{1,3,2,0:T(8,128)S(1)} fusion(bf16[4,256,4,64]{1,3,2,0:T(8,128)(2,1)S(1)} %copy.82, f32[4,4,256]{2,0,1:T(4,128)S(1)} %bitcast.108, f32[4,256,256]{2,1,0:T(8,128)S(1)} %fusion.50, f32[4,4,256]{2,0,1:T(4,128)S(1)} %copy-done.9, pred[4,256,256]{2,1,0:T(8,128)(4,1)} %compare_and_fusion), kind=kOutput, calls=%fused_computation.11 | convolution fusion | flops 140509184 | bytes 2916352 | tf_op jit(solution)/shard_map/hcts,cshp->cthp/dot_general | solution.py:83
  106.9 8.2 %all-to-all-done.1 = bf16[16,8,512]{2,1,0:T(8,128)(2,1)S(1)} async-done(((bf16[16,8,512]{2,1,0:T(8,128)(2,1)}), bf16[16,8,512]{2,1,0:T(8,128)(2,1)S(1)}, u32[]{:S(2)}, u32[]{:S(2)}) %all-to-all-start.1) | async-done | bytes 131104 | tf_op jit(solution)/shard_map/all_to_all | solution.py:48
  117.3 24.7 %all_to_all.15 = bf16[64,8,128]{2,1,0:T(8,128)(2,1)S(1)} all-to-all(bf16[64,8,128]{2,1,0:T(8,128)(2,1)S(1)} %broadcast_in_dim.32), channel_id=1, replica_groups=mesh['context'=16,'head'=64] {'head'}, dimensions={0} | all-to-all | bytes 262144 | tf_op jit(solution)/shard_map/all_to_all | solution.py:56
  (145 shorter events, 27.4 us)
Async XLA Ops:
  0.0 7.4 %copy-start.20 = (s32[64]{0:T(128)S(1)}, s32[64]{0:T(128)}, u32[]{:S(2)}) copy-start(s32[64]{0:T(128)} %param.25) | copy-start | bytes 772
  0.0 8.1 %copy-start.23 = (f32[4]{0:T(128)S(1)}, f32[4]{0:T(128)}, u32[]{:S(2)}) copy-start(f32[4]{0:T(128)} %param.22) | copy-start | bytes 52
  0.0 8.1 %copy-start.10 = (bf16[4,1024]{1,0:T(4,128)(2,1)S(1)}, bf16[4,1024]{1,0:T(4,128)(2,1)}, u32[]{:S(2)}) copy-start(bf16[4,1024]{1,0:T(4,128)(2,1)} %param.16) | copy-start | bytes 24580
  0.0 8.1 %copy-start.21 = (f32[4]{0:T(128)S(1)}, f32[4]{0:T(128)}, u32[]{:S(2)}) copy-start(f32[4]{0:T(128)} %param.21) | copy-start | bytes 52
  0.0 17.3 %copy-start.17 = (f32[4,256]{1,0:T(4,128)S(1)}, f32[4,256]{1,0:T(4,128)}, u32[]{:S(2)}) copy-start(f32[4,256]{1,0:T(4,128)} %param.17) | copy-start | bytes 12292
  0.0 18.4 %copy-start.19 = (f32[256]{0:T(256)S(1)}, f32[256]{0:T(256)}, u32[]{:S(2)}) copy-start(f32[256]{0:T(256)} %param.18) | copy-start | bytes 3076
  1.4 20.4 %copy-start = (bf16[1024,256]{1,0:T(8,128)(2,1)S(1)}, bf16[1024,256]{1,0:T(8,128)(2,1)}, u32[]{:S(2)}) copy-start(bf16[1024,256]{1,0:T(8,128)(2,1)} %param.13) | copy-start | bytes 1572868
  2.6 19.2 %collective-permute-start = (bf16[3,768]{1,0:T(4,128)(2,1)S(1)}, bf16[3,768]{1,0:T(4,128)(2,1)S(1)}, u32[]{:S(2)}, u32[]{:S(2)}) collective-permute-start(bf16[3,768]{1,0:T(4,128)(2,1)S(1)} %slice.273), channel_id=1, source_target_pairs={{0,64},{64,128},{128,192},{192,256},{256,320},{320,384},{384,448},... | collective-permute-start | bytes 13832 | tf_op jit(solution)/shard_map/ppermute | solution.py:19
  16.5 5.6 %copy-start.11 = (f32[4]{0:T(128)}, f32[4]{0:T(128)S(1)}, u32[]{:S(2)}) copy-start(f32[4]{0:T(128)S(1)} %get-tuple-element.11) | copy-start | bytes 52
  16.6 5.6 %copy-start.13 = (f32[4]{0:T(128)}, f32[4]{0:T(128)S(1)}, u32[]{:S(2)}) copy-start(f32[4]{0:T(128)S(1)} %get-tuple-element.14) | copy-start | bytes 52
  16.6 5.6 %copy-start.15 = (f32[4]{0:T(128)}, f32[4]{0:T(128)S(1)}, u32[]{:S(2)}) copy-start(f32[4]{0:T(128)S(1)} %get-tuple-element.15) | copy-start | bytes 52
  18.2 4.1 %copy-start.6 = (s32[4,256]{1,0:T(4,128)}, s32[4,256]{1,0:T(4,128)S(1)}, u32[]{:S(2)}) copy-start(s32[4,256]{1,0:T(4,128)S(1)} %eq.70) | copy-start | bytes 12292
  25.2 1.1 copy-start.5
  26.6 3.9 %copy-start.2 = (f32[16,8,512]{2,1,0:T(8,128)S(1)}, f32[16,8,512]{2,1,0:T(8,128)}, u32[]{:S(2)}) copy-start(f32[16,8,512]{2,1,0:T(8,128)} %mul.573) | copy-start | bytes 786436
  30.5 23.1 %copy-start.7 = (s32[4,256]{1,0:T(4,128)S(1)}, s32[4,256]{1,0:T(4,128)}, u32[]{:S(2)}) copy-start(s32[4,256]{1,0:T(4,128)} %copy-done.6) | copy-start | bytes 12292
  31.7 71.8 %copy-start.9 = (f32[4,4,256]{2,0,1:T(4,128)S(1)}, f32[4,4,256]{2,0,1:T(4,128)}, u32[]{:S(2)}) copy-start(f32[4,4,256]{2,0,1:T(4,128)} %get-tuple-element.52) | copy-start | bytes 49156
  33.1 29.8 %all-to-all-start = ((bf16[16,8,640]{2,1,0:T(8,128)(2,1)}), bf16[16,8,640]{2,1,0:T(8,128)(2,1)S(1)}, u32[]{:S(2)}, u32[]{:S(2)}) async-start(bf16[16,8,640]{2,1,0:T(8,128)(2,1)} %pad_maximum_fusion.1), calls=%async_computation | async-start | bytes 327680 | tf_op jit(solution)/shard_map/all_to_all | solution.py:38
  63.0 3.4 %copy-start.1 = (f32[16,8,640]{2,1,0:T(8,128)}, f32[16,8,640]{2,1,0:T(8,128)S(1)}, u32[]{:S(2)}) copy-start(f32[16,8,640]{2,1,0:T(8,128)S(1)} %convert_element_type.187) | copy-start | bytes 983044
  95.6 19.5 %all-to-all-start.1 = ((bf16[16,8,512]{2,1,0:T(8,128)(2,1)}), bf16[16,8,512]{2,1,0:T(8,128)(2,1)S(1)}, u32[]{:S(2)}, u32[]{:S(2)}) async-start(bf16[16,8,512]{2,1,0:T(8,128)(2,1)} %constant_dynamic-update-slice_fusion), calls=%async_computation.1 | async-start | bytes 262144 | tf_op jit(solution)/shard_map/all_to_all | solution.py:48
  103.5 12.0 %copy-start.3 = (bf16[1,4,64,256]{3,2,1,0:T(8,128)(2,1)S(1)}, bf16[1,4,64,256]{3,2,1,0:T(8,128)(2,1)}, u32[]{:S(2)}) copy-start(bf16[1,4,64,256]{3,2,1,0:T(8,128)(2,1)} %get-tuple-element.42) | copy-start | bytes 393220
  103.5 12.0 %copy-start.4 = (bf16[1,4,64,256]{3,2,1,0:T(8,128)(2,1)S(1)}, bf16[1,4,64,256]{3,2,1,0:T(8,128)(2,1)}, u32[]{:S(2)}) copy-start(bf16[1,4,64,256]{3,2,1,0:T(8,128)(2,1)} %get-tuple-element.43) | copy-start | bytes 393220
  103.5 12.0 %copy-start.8 = (f32[4,256,4]{1,2,0:T(4,128)S(1)}, f32[4,256,4]{1,2,0:T(4,128)}, u32[]{:S(2)}) copy-start(f32[4,256,4]{1,2,0:T(4,128)} %get-tuple-element.50) | copy-start | bytes 49156
  103.5 12.0 %copy-start.22 = (f32[4]{0:T(128)S(1)}, f32[4]{0:T(128)}, u32[]{:S(2)}) copy-start(f32[4]{0:T(128)} %param.23) | copy-start | bytes 52
  116.0 26.1 %copy-start.18 = (f32[256]{0:T(256)S(1)}, f32[256]{0:T(256)}, u32[]{:S(2)}) copy-start(f32[256]{0:T(256)} %param.24) | copy-start | bytes 3076
  (3 other events, 2.1 us)

commit v2 on v0

v2 whole, which is shorter than its diff:
```python
import functools

import jax
import jax.numpy as jnp
from jax import lax
from jax.experimental import pallas as pl
from jax.experimental.pallas import tpu as pltpu
from jax.sharding import PartitionSpec as P

HEAD_DIM = 64
STATE = 256
GROUPS = 8
CONV = 4
BLOCK = 256
HALO = 8

norm_floor = 1e-05
f32 = jnp.float32
bf16 = jnp.bfloat16
exact_mode = lax.Precision.HIGHEST


def dot(left, right, precision=None):
    return jnp.dot(left, right, preferred_element_type=f32, precision=precision)


def dot_rows(left, right, precision=None):
    return lax.dot_general(
        left, right, (((1,), (1,)), ((), ())), preferred_element_type=f32, precision=precision
    )


def iota(shape, axis):
    return lax.broadcasted_iota(jnp.int32, shape, axis)


def silu(value):
    half = 0.5 * value
    return half + half * jnp.tanh(half)


def split_pair(value):
    high = value.astype(bf16)
    return high, (value - high.astype(f32)).astype(bf16)


def doc_starts(doc_len, first):
    count = doc_len.shape[1]
    lengths = doc_len.astype(f32)
    row, column = iota((count, count), 0), iota((count, count), 1)
    down = jnp.sum(jnp.where(row == column, lengths, 0.0), axis=1, keepdims=True)
    begins = jnp.sum(jnp.where(row < column, down, 0.0), axis=0, keepdims=True)
    places = (iota((BLOCK, 1), 0) + first).astype(f32)
    starts = jnp.max(jnp.where(begins <= places, begins, -1.0), axis=1, keepdims=True)
    return starts, places


def steps(dt, dt_bias, a_log):
    heads = dt.shape[0]
    values = jnp.concatenate([dt.astype(f32)] * (8 // heads), axis=0)
    row = iota((8, 1), 0) % heads
    bias = jnp.zeros((8, 1), f32)
    log_rate = jnp.zeros((8, 1), f32)
    for head in range(heads):
        bias = jnp.where(row == head, dt_bias[head], bias)
        log_rate = jnp.where(row == head, a_log[head], log_rate)
    values = values + bias
    step = jnp.maximum(values, 0.0) + jnp.log1p(jnp.exp(-jnp.abs(values)))
    return step, step * -jnp.exp(log_rate)


def conv_silu(block, ext, before, raw, weights, bias, age):
    @pl.when(block == 0)
    def _():
        ext[0:HALO] = before.astype(f32)

    @pl.when(block > 0)
    def _():
        ext[0:HALO] = ext[BLOCK : BLOCK + HALO]

    now = raw.astype(f32)
    ext[HALO : HALO + BLOCK] = now
    summed = bias + weights[CONV - 1 : CONV] * now
    for back in range(1, CONV):
        kept = jnp.where(age >= back, 1.0, 0.0)
        older = ext[HALO - back : HALO - back + BLOCK]
        summed = summed + weights[CONV - 1 - back : CONV - back] * (older * kept)
    return silu(summed).astype(bf16)


def wide_row(ref, at):
    return jnp.concatenate([ref[pl.ds(at, 1), :], ref[pl.ds(at + 1, 1), :]], axis=1)


def ends_kernel(
    place, x_in, b_in, halo, dt_in, x_w, x_b, b_w, b_b, dt_bias, a_log, doc_len,
    x_out, b_out, states_out, sent, ext_x, ext_b, state, total,
):
    block = pl.program_id(0)
    blocks = pl.num_programs(0)
    group, first = place[0], place[1]
    start, places = doc_starts(doc_len[...], first + block * BLOCK)
    age = places - start
    width = x_in.shape[1]
    x = conv_silu(block, ext_x, halo[:, :width], x_in[...], x_w[...], wide_row(x_b, 0), age)
    b = conv_silu(
        block, ext_b, halo[:, width : width + STATE], b_in[...], b_w[...],
        wide_row(b_b, 2 * group), age,
    )
    x_out[...] = x
    b_out[...] = b
    step, decay = steps(dt_in[...], dt_bias, a_log)
    upto = (iota((BLOCK, BLOCK), 0) <= iota((BLOCK, BLOCK), 1)).astype(f32)
    running = dot(decay, upto, exact_mode)
    last = running[:, BLOCK - 1 : BLOCK]
    last_start = start[BLOCK - 1 : BLOCK]
    ahead = (iota((1, BLOCK), 1) + first + block * BLOCK).astype(f32)
    tail = jnp.where(ahead >= last_start, jnp.exp(last - running), 0.0) * step
    block_start = (first + block * BLOCK).astype(f32)
    carry = jnp.where(last_start < block_start, jnp.exp(last), 0.0)

    @pl.when(block == 0)
    def _():
        state[...] = jnp.zeros_like(state)
        total[...] = jnp.zeros_like(total)

    heads = dt_in.shape[0]
    old = state[...]
    states_out[0] = old.astype(bf16)
    across = jnp.transpose(x.astype(f32))
    scaled, kept = [], []
    for head in range(heads):
        rows = slice(head * HEAD_DIM, (head + 1) * HEAD_DIM)
        scaled.append(across[rows] * tail[head : head + 1])
        kept.append(old[rows] * carry[head : head + 1])
    high, low = split_pair(jnp.concatenate(scaled, axis=0))
    new = jnp.concatenate(kept, axis=0) + dot(high, b) + dot(low, b)
    state[...] = new
    total[...] = total[...] + last

    @pl.when(block == blocks - 1)
    def _():
        count = sent.shape[0]
        shard_start = first.astype(f32)
        through = jnp.where(last_start < shard_start, jnp.exp(total[...]), 0.0)
        top = through.astype(bf16).astype(f32)
        middle = (through - top).astype(bf16).astype(f32)
        rest = through - top - middle
        lane = iota((8, 128), 1)
        for piece in range(count):
            rows = 2 * HALO * piece
            head = piece * heads // count
            sent[piece, :, :STATE] = new[rows : rows + HALO].astype(bf16)
            sent[piece, :, STATE : 2 * STATE] = new[rows + HALO : rows + 2 * HALO].astype(bf16)
            one = slice(head, head + 1)
            extra = jnp.where(lane == 0, top[one], jnp.where(lane == 1, middle[one], rest[one]))
            sent[piece, :, 2 * STATE :] = extra.astype(bf16)


def spread(columns):
    lane = iota((BLOCK, 128), 1)
    return jnp.concatenate(
        [
            jnp.where(lane < HEAD_DIM, columns[:, at : at + 1], columns[:, at + 1 : at + 2])
            for at in (0, 2)
        ],
        axis=1,
    )


def inside_kernel(
    place, x_ref, b_ref, c_in, z_in, halo, dt_in, c_w, c_b, states, dt_bias, a_log, skip, doc_len,
    c_out, base_out, gain_out, ext_c, total,
):
    block = pl.program_id(0)
    group, first = place[0], place[1]
    start, places = doc_starts(doc_len[...], first + block * BLOCK)
    c = conv_silu(
        block, ext_c, halo[:, 2 * STATE : 3 * STATE], c_in[...], c_w[...],
        wide_row(c_b, 2 * (GROUPS + group)), places - start,
    )
    c_out[...] = c
    step, decay = steps(dt_in[...], dt_bias, a_log)
    older = iota((BLOCK, BLOCK), 1) <= iota((BLOCK, BLOCK), 0)
    tri = older.astype(f32)
    down = dot_rows(tri, decay, exact_mode)
    running = dot_rows(decay, tri, exact_mode)
    ahead = (iota((1, BLOCK), 1) + first + block * BLOCK).astype(f32)
    same = older & (ahead >= start)
    inner = dot_rows(c, b_ref[...])
    x = x_ref[...]
    x_wide = x.astype(f32)
    column = iota((BLOCK, x.shape[1]), 1)
    heads = dt_in.shape[0]
    y = jnp.zeros((BLOCK, x.shape[1]), f32)
    gains = jnp.zeros((1, x.shape[1]), f32)
    for head in range(heads):
        gap = jnp.minimum(down[:, head : head + 1] - running[head : head + 1], 0.0)
        mixing = jnp.where(same, jnp.exp(gap), 0.0) * step[head : head + 1] * inner
        own = (column >= head * HEAD_DIM) & (column < (head + 1) * HEAD_DIM)
        y = y + dot(mixing.astype(bf16), jnp.where(own, x_wide, 0.0).astype(bf16))
        gains = jnp.where(own[0:1], skip[head], gains)

    @pl.when(block == 0)
    def _():
        total[...] = jnp.zeros_like(total)

    block_start = (first + block * BLOCK).astype(f32)
    local = jnp.where(start < block_start, jnp.exp(down), 0.0)
    far = jnp.where(start < first.astype(f32), jnp.exp(down + total[...]), 0.0)
    total[...] = total[...] + down[BLOCK - 1 : BLOCK]
    y = y + dot_rows(c, states[0]) * spread(local) + gains * x_wide
    gate = silu(z_in[...].astype(f32))
    base_out[...] = y * gate
    gain_out[...] = spread(far) * gate


def scan_kernel(got, back):
    now = jnp.zeros((HALO, 2 * STATE), f32)
    for shard in range(got.shape[0]):
        back[shard] = now.astype(bf16)
        message = got[shard].astype(f32)
        at = 2 * STATE
        factor = message[0:1, at : at + 1] + message[0:1, at + 1 : at + 2]
        factor = factor + message[0:1, at + 2 : at + 3]
        now = factor * now + message[:, :at]


def join_kernel(mine, c_ref, base, gain, gated_out, copies, entering, squares):
    block = pl.program_id(0)

    @pl.when(block == 0)
    def _():
        rows = []
        for piece in range(mine.shape[0]):
            part = mine[piece].astype(f32)
            rows += [part[:, :STATE], part[:, STATE:]]
        entering[...] = jnp.concatenate(rows, axis=0).astype(bf16)

    gated = base[...] + gain[...] * dot_rows(c_ref[...], entering[...])
    gated_out[...] = gated
    high, low = split_pair(gated * gated)
    ones = jnp.ones((8, gated.shape[1]), bf16)
    sums = dot_rows(ones, high) + dot_rows(ones, low)
    squares[pl.ds(2 * block, 1), :] = sums[0:1, :128]
    squares[pl.ds(2 * block + 1, 1), :] = sums[0:1, 128:]

    @pl.when(block == pl.num_programs(0) - 1)
    def _():
        copies[...] = jnp.broadcast_to(squares[...].astype(bf16)[None], copies.shape)


def finish_kernel(channels, everything, gated, norm, out, scale):
    block = pl.program_id(0)

    @pl.when(block == 0)
    def _():
        total = jnp.sum(everything[...].astype(f32), axis=0)
        scale[...] = lax.rsqrt(total / channels + norm_floor)

    same = iota((128, 128), 0) == iota((128, 128), 1)
    columns = []
    for half in range(2):
        row = scale[pl.ds(2 * block + half, 1), :]
        columns.append(jnp.sum(jnp.where(same, row, 0.0), axis=1, keepdims=True))
    column = jnp.concatenate(columns, axis=0)
    out[...] = (gated[...] * column * wide_row(norm, 0)).astype(bf16)


def shards(
    x_in, bc_in, z_in, dt_in, conv_x_w, conv_x_b, conv_bc_w, conv_bc_b, dt_bias, a_log,
    skip_gain, norm_w, doc_len,
):
    rows, width = x_in.shape
    heads = dt_in.shape[0]
    heads_total = heads * lax.axis_size("head")
    per_group = heads_total // GROUPS
    group = lax.axis_index("head") * heads // per_group
    place = jnp.stack([group, lax.axis_index("context") * rows]).astype(jnp.int32)
    shard_count = lax.axis_size("context")
    head_count = lax.axis_size("head")
    blocks = rows // BLOCK

    bc_last = bc_in[rows - HALO :]
    last = jnp.concatenate(
        [
            x_in[rows - HALO :],
            lax.dynamic_slice_in_dim(bc_last, group * STATE, STATE, 1),
            lax.dynamic_slice_in_dim(bc_last, (GROUPS + group) * STATE, STATE, 1),
        ],
        axis=1,
    )
    pairs = [(i, i + 1) for i in range(shard_count - 1)]
    halo = lax.ppermute(last, "context", pairs)
    x_b = conv_x_b.reshape(-1, 128)
    bc_b = conv_bc_b.reshape(-1, 128)
    norm = norm_w.reshape(-1, 128)
    docs = doc_len.reshape(1, -1)

    def whole(*shape):
        return pl.BlockSpec(shape, lambda i, *_: (0,) * len(shape))

    tokens = pl.BlockSpec((BLOCK, width), lambda i, *_: (i, 0))
    b_cols = pl.BlockSpec((BLOCK, STATE), lambda i, s: (i, s[0]))
    c_cols = pl.BlockSpec((BLOCK, STATE), lambda i, s: (i, s[0] + GROUPS))
    b_taps = pl.BlockSpec((CONV, STATE), lambda i, s: (0, s[0]))
    c_taps = pl.BlockSpec((CONV, STATE), lambda i, s: (0, s[0] + GROUPS))
    dt_cols = pl.BlockSpec((heads, BLOCK), lambda i, *_: (0, i))
    scalars = pl.BlockSpec(memory_space=pltpu.SMEM)
    block_states = pl.BlockSpec((1, width, STATE), lambda i, *_: (i, 0, 0))

    def call(kernel, prefetch, in_specs, out_specs, out_shape, scratch, grid=(blocks,), cost=5e8):
        return pl.pallas_call(
            kernel,
            grid_spec=pltpu.PrefetchScalarGridSpec(
                num_scalar_prefetch=prefetch,
                grid=grid,
                in_specs=in_specs,
                out_specs=out_specs,
                scratch_shapes=scratch,
            ),
            out_shape=out_shape,
            cost_estimate=pl.CostEstimate(
                flops=int(cost), bytes_accessed=4_000_000, transcendentals=1_000_000
            ),
        )

    struct = jax.ShapeDtypeStruct
    message = 2 * STATE + 128
    x, b, states, sent = call(
        ends_kernel,
        1,
        [
            tokens, b_cols, whole(HALO, width + 2 * STATE), dt_cols, whole(CONV, width),
            whole(*x_b.shape), b_taps, whole(*bc_b.shape), scalars, scalars, whole(*docs.shape),
        ],
        [tokens, tokens, block_states, whole(shard_count, HALO, message)],
        [
            struct((rows, width), bf16),
            struct((rows, STATE), bf16),
            struct((blocks, width, STATE), bf16),
            struct((shard_count, HALO, message), bf16),
        ],
        [
            pltpu.VMEM((BLOCK + HALO, width), f32),
            pltpu.VMEM((BLOCK + HALO, STATE), f32),
            pltpu.VMEM((width, STATE), f32),
            pltpu.VMEM((8, 1), f32),
        ],
    )(place, x_in, bc_in, halo, dt_in, conv_x_w, x_b, conv_bc_w, bc_b, dt_bias, a_log, docs)
    got = lax.all_to_all(sent, "context", split_axis=0, concat_axis=0, tiled=True)
    c, base, gain = call(
        inside_kernel,
        1,
        [
            tokens, tokens, c_cols, tokens, whole(HALO, width + 2 * STATE), dt_cols, c_taps,
            whole(*bc_b.shape), block_states, scalars, scalars, scalars, whole(*docs.shape),
        ],
        [tokens, tokens, tokens],
        [
            struct((rows, STATE), bf16),
            struct((rows, width), f32),
            struct((rows, width), f32),
        ],
        [pltpu.VMEM((BLOCK + HALO, STATE), f32), pltpu.VMEM((1, 8), f32)],
    )(
        place, x, b, bc_in, z_in, halo, dt_in, conv_bc_w, bc_b, states, dt_bias, a_log,
        skip_gain, docs,
    )
    back = pl.pallas_call(
        scan_kernel, out_shape=struct((shard_count, HALO, 2 * STATE), bf16)
    )(got)
    mine = lax.all_to_all(back, "context", split_axis=0, concat_axis=0, tiled=True)
    gated, copies = call(
        join_kernel,
        0,
        [whole(shard_count, HALO, 2 * STATE), tokens, tokens, tokens],
        [tokens, whole(head_count, rows // 128, 128)],
        [struct((rows, width), f32), struct((head_count, rows // 128, 128), bf16)],
        [pltpu.VMEM((width, STATE), bf16), pltpu.VMEM((rows // 128, 128), f32)],
    )(mine, c, base, gain)
    everything = lax.all_to_all(copies, "head", split_axis=0, concat_axis=0, tiled=True)
    return call(
        functools.partial(finish_kernel, float(heads_total * HEAD_DIM)),
        0,
        [whole(head_count, rows // 128, 128), tokens, whole(*norm.shape)],
        tokens,
        struct((rows, width), bf16),
        [pltpu.VMEM((rows // 128, 128), f32)],
    )(everything, gated, norm)


def solution(mesh):
    return jax.shard_map(
        shards,
        mesh=mesh,
        in_specs=(
            P("context", "head"),
            P("context", None),
            P("context", "head"),
            P("head", "context"),
            P(None, "head"),
            P("head"),
            P(),
            P(),
            P("head"),
            P("head"),
            P("head"),
            P("head"),
            P(),
        ),
        out_specs=P("context", "head"),
        check_vma=False,
    )
```

time: 162 us -> 103 us (0.64); the launches traced: 159 us -> 102 us
  waiting for transfers between devices: 34.9 us -> 2.69 us
  Pallas kernels: 0 us -> 27.9 us
  other arithmetic: 17.6 us -> 0.61 us
  between operations: 14.5 us -> 0.04 us
  matrix products: 10.6 us -> 0 us
  blocking collectives: 65.9 us -> 57.1 us
  local copies, waits for them, and re-layouts: 10.9 us -> 2.78 us
  starting transfers between devices: 4.85 us -> 11.3 us
    all_gather x1 -> x0, waiting for transfers between devices: 34.9 us -> none  [entering_2(): gathered = jax.tree.map(lambda a: lax.all_gather(a, axis), part)]
    unnamed x1 -> x0, blocking collectives: 33.9 us -> none
    pallas_call x0 -> x5, Pallas kernels: none -> 27.9 us  [the longest x1 9.48 us: shards(): call(inside_kernel, 1, [tokens, tokens, c_cols, tokens, whole(HALO, width...]
    all_to_all x1 -> x2, blocking collectives: 31.9 us -> 57.1 us  [the longest x1 31.6 us: shards(): lax.all_to_all(sent, 'context', split_axis=0, concat_axis=0, tiled=True)]
    dot_general x4 -> x0, matrix products: 10.6 us -> none  [the longest x1 7.13 us: shards(): jnp.einsum('hcts,cshp->cthp', mixing, weighted, precision=exact_mode)]
    all_to_all x0 -> x1, starting transfers between devices: none -> 6.47 us  [shards(): lax.all_to_all(back, 'context', split_axis=0, concat_axis=0, tiled=True)]
    another operation x8 -> x1, other arithmetic: 6.38 us -> 0.61 us  [shards(): jnp.stack([group, lax.axis_index('context') * rows]).astype(jnp.int32)]
    convert_element_type x5 -> x0, other arithmetic: 3.61 us -> none  [the longest x1 2.97 us: conv_silu(): return jax.nn.silu(summed).astype(jnp.bfloat16)]
  transfers between devices with their start and end apart: 2 -> 2, of which waited for: 1 -> 2; matrix products, arithmetic and copies ran while one was open for 13% -> 1% of each run, Pallas kernels for 0% -> 9%
where the time goes in v2:
time: 103 us; the launch traced here: 102 us
  blocking collectives  57.1 us (55%)
  Pallas kernels  27.9 us (27%)
  starting transfers between devices  11.3 us (11%)
  local copies, waits for them, and re-layouts  2.78 us (3%)
  waiting for transfers between devices  2.69 us (3%)
    all_to_all x1, blocking collectives, shards(): lax.all_to_all(sent, 'context', split_axis=0, concat_axis=0, tiled=True)  31.6 us
    all_to_all x1, blocking collectives, shards(): lax.all_to_all(copies, 'head', split_axis=0, concat_axis=0, tiled=True)  25.5 us
    pallas_call x1, Pallas kernels, shards(): call(inside_kernel, 1, [tokens, tokens, c_cols, tokens, whole(HALO, width...  9.48 us
    pallas_call x1, Pallas kernels, shards(): call(ends_kernel, 1, [tokens, b_cols, whole(HALO, width + 2 * STATE), dt_...  8.27 us
    all_to_all x1, starting transfers between devices, shards(): lax.all_to_all(back, 'context', split_axis=0, concat_axis=0, tiled=True)  6.47 us
    ppermute x1, starting transfers between devices, shards(): halo = lax.ppermute(last, 'context', pairs)  4.81 us
    pallas_call x1, Pallas kernels, shards(): call(join_kernel, 0, [whole(shard_count, HALO, 2 * STATE), tokens, tokens...  4.71 us
    pallas_call x1, Pallas kernels, shards(): call(functools.partial(finish_kernel, float(heads_total * HEAD_DIM)), 0,...  3.78 us
  transfers between devices with their start and end apart: 2, of which 2 were waited for; matrix products, arithmetic and copies ran while one was open for 1% of the time, Pallas kernels for 9%

profile of v2, /device:TPU:1, one launch (start us, length us, event | category | flops | bytes accessed | tf_op | source)
XLA Modules:
  0.0 102.5 jit_solution(562953356770548113)
XLA Ops:
  0.0 0.7 slice.6
  0.7 0.8 slice.7
  1.5 4.8 %collective-permute-start = (bf16[8,768]{1,0:T(8,128)(2,1)S(1)}, bf16[8,768]{1,0:T(8,128)(2,1)S(1)}, u32[]{:S(2)}, u32[]{:S(2)}) collective-permute-start(bf16[8,768]{1,0:T(8,128)(2,1)S(1)} %pad_maximum_fusion), channel_id=1, source_target_pairs={{0,64},{64,128},{128,192},{192,256},{256,320},{320,384},{384,448},... | collective-permute-start | bytes 36872 | tf_op jit(solution)/shard_map/ppermute | solution.py:294
  6.4 0.6 pad_add_fusion.place
  7.0 0.2 collective-permute-done.halo
  7.2 0.0 copy-start.1
  7.2 0.6 copy-done.1
  7.8 8.3 %shard_map.127 = (bf16[1024,256]{1,0:T(8,128)(2,1)}, bf16[1024,256]{1,0:T(8,128)(2,1)}, bf16[4,256,256]{2,1,0:T(8,128)(2,1)}, bf16[16,8,640]{2,1,0:T(8,128)(2,1)}) custom-call(s32[2]{0:T(128)} %pad_add_fusion.place, bf16[1024,256]{1,0:T(8,128)(2,1)} %x_in.1, bf16[1024,4096]{1,0:T(8,128)(2,1)} %c_in.1, bf16[8,768]{1,0:T(8,128)(2,1)} %copy-done.1, ...), custom_call_target="tpu_custom_call" | custom-call | flops 500000000 | bytes 4000000 | tf_op jit(solution)/shard_map/pallas_call | solution.py:330
  16.0 31.6 %all_to_all.15.got = bf16[16,8,640]{2,1,0:T(8,128)(2,1)} all-to-all(bf16[16,8,640]{2,1,0:T(8,128)(2,1)} %get-tuple-element.14), channel_id=1, replica_groups=mesh['context'=16,'head'=64] {'context'}, dimensions={0} | all-to-all | bytes 327680 | tf_op jit(solution)/shard_map/all_to_all | solution.py:351
  47.7 1.7 %shard_map.128 = bf16[16,8,512]{2,1,0:T(8,128)(2,1)} custom-call(bf16[16,8,640]{2,1,0:T(8,128)(2,1)} %all_to_all.15.got), custom_call_target="tpu_custom_call" | custom-call | tf_op jit(solution)/shard_map/pallas_call | solution.py:370
  49.4 6.5 %all-to-all-start.1 = ((bf16[16,8,512]{2,1,0:T(8,128)(2,1)}), bf16[16,8,512]{2,1,0:T(8,128)(2,1)S(1)}, u32[]{:S(2)}, u32[]{:S(2)}) async-start(bf16[16,8,512]{2,1,0:T(8,128)(2,1)} %shard_map.128), calls=%async_computation.1 | async-start | bytes 262144 | tf_op jit(solution)/shard_map/all_to_all | solution.py:373
  55.9 9.5 %shard_map.129 = (bf16[1024,256]{1,0:T(8,128)(2,1)}, f32[1024,256]{1,0:T(8,128)}, f32[1024,256]{1,0:T(8,128)}) custom-call(s32[2]{0:T(128)} %pad_add_fusion.place, bf16[1024,256]{1,0:T(8,128)(2,1)} %get-tuple-element.15.x_ref, bf16[1024,256]{1,0:T(8,128)(2,1)} %get-tuple-element.16.b_ref, bf16[1024,4096]{1,0:T(8,128)(2,1)} %c_in.1, bf16[1024,256]{1,0:T(8,128)(2,1)} %z_in.1, ...), custom_call_target="tpu_custom_call" | custom-call | flops 500000000 | bytes 4000000 | tf_op jit(solution)/shard_map/pallas_call | solution.py:352
  65.3 2.5 %all-to-all-done.1.mine = bf16[16,8,512]{2,1,0:T(8,128)(2,1)S(1)} async-done(((bf16[16,8,512]{2,1,0:T(8,128)(2,1)}), bf16[16,8,512]{2,1,0:T(8,128)(2,1)S(1)}, u32[]{:S(2)}, u32[]{:S(2)}) %all-to-all-start.1) | async-done | bytes 131104 | tf_op jit(solution)/shard_map/all_to_all | solution.py:373
  67.8 0.0 copy-start
  67.8 0.7 copy-done
  68.5 4.7 %shard_map.130 = (f32[1024,256]{1,0:T(8,128)}, bf16[64,8,128]{2,1,0:T(8,128)(2,1)}) custom-call(bf16[16,8,512]{2,1,0:T(8,128)(2,1)} %copy-done, bf16[1024,256]{1,0:T(8,128)(2,1)} %get-tuple-element.18.c_ref, f32[1024,256]{1,0:T(8,128)} %get-tuple-element.19.base, f32[1024,256]{1,0:T(8,128)} %get-tuple-element.20.gain), custom_call_target="tpu_custom_call" | custom-call | flops 500000000 | bytes 4000000 | tf_op jit(solution)/shard_map/pallas_call | solution.py:374
  73.2 25.5 %all_to_all.16.everything = bf16[64,8,128]{2,1,0:T(8,128)(2,1)} all-to-all(bf16[64,8,128]{2,1,0:T(8,128)(2,1)} %get-tuple-element.21), channel_id=1, replica_groups=mesh['context'=16,'head'=64] {'head'}, dimensions={0} | all-to-all | bytes 262144 | tf_op jit(solution)/shard_map/all_to_all | solution.py:382
  98.7 3.8 %shard_map.131 = bf16[1024,256]{1,0:T(8,128)(2,1)} custom-call(bf16[64,8,128]{2,1,0:T(8,128)(2,1)} %all_to_all.16.everything, f32[1024,256]{1,0:T(8,128)} %get-tuple-element.22.gated, f32[2,128]{1,0:T(2,128)} %bitcast.11), custom_call_target="tpu_custom_call" | custom-call | flops 500000000 | bytes 4000000 | tf_op jit(solution)/shard_map/pallas_call | solution.py:383
  (2 shorter events, 0.0 us)
Async XLA Ops:
  1.5 5.6 %collective-permute-start = (bf16[8,768]{1,0:T(8,128)(2,1)S(1)}, bf16[8,768]{1,0:T(8,128)(2,1)S(1)}, u32[]{:S(2)}, u32[]{:S(2)}) collective-permute-start(bf16[8,768]{1,0:T(8,128)(2,1)S(1)} %pad_maximum_fusion), channel_id=1, source_target_pairs={{0,64},{64,128},{128,192},{192,256},{256,320},{320,384},{384,448},... | collective-permute-start | bytes 36872 | tf_op jit(solution)/shard_map/ppermute | solution.py:294
  7.2 0.6 copy-start.1
  49.4 18.5 %all-to-all-start.1 = ((bf16[16,8,512]{2,1,0:T(8,128)(2,1)}), bf16[16,8,512]{2,1,0:T(8,128)(2,1)S(1)}, u32[]{:S(2)}, u32[]{:S(2)}) async-start(bf16[16,8,512]{2,1,0:T(8,128)(2,1)} %shard_map.128), calls=%async_computation.1 | async-start | bytes 262144 | tf_op jit(solution)/shard_map/all_to_all | solution.py:373
  67.8 0.7 copy-start

commit v3 on v2

--- a/solution.py
+++ b/solution.py
@@ -13,6 +13,8 @@
 CONV = 4
 BLOCK = 256
 HALO = 8
+GRANT = 16 * 1024 * 1024
+WIDE_GRANT = 46 * 1024 * 1024
 
 norm_floor = 1e-05
 f32 = jnp.float32
@@ -94,17 +96,33 @@
 
 def ends_kernel(
     place, x_in, b_in, halo, dt_in, x_w, x_b, b_w, b_b, dt_bias, a_log, doc_len,
-    x_out, b_out, states_out, sent, ext_x, ext_b, state, total,
+    x_out, b_out, states_out, sent, ext_x, ext_b, state, total, x_raw, b_raw, arrived,
 ):
     block = pl.program_id(0)
     blocks = pl.num_programs(0)
     group, first = place[0], place[1]
+    columns = pl.ds(pl.multiple_of(group * STATE, STATE), STATE)
+    copies = (
+        pltpu.make_async_copy(x_in, x_raw, arrived.at[0]),
+        pltpu.make_async_copy(b_in.at[:, columns], b_raw, arrived.at[1]),
+    )
+
+    @pl.when(block == 0)
+    def _():
+        for copy in copies:
+            copy.start()
+        state[...] = jnp.zeros_like(state)
+        total[...] = jnp.zeros_like(total)
+        for copy in copies:
+            copy.wait()
+
+    here = pl.ds(pl.multiple_of(block * BLOCK, BLOCK), BLOCK)
     start, places = doc_starts(doc_len[...], first + block * BLOCK)
     age = places - start
     width = x_in.shape[1]
-    x = conv_silu(block, ext_x, halo[:, :width], x_in[...], x_w[...], wide_row(x_b, 0), age)
+    x = conv_silu(block, ext_x, halo[:, :width], x_raw[here], x_w[...], wide_row(x_b, 0), age)
     b = conv_silu(
-        block, ext_b, halo[:, width : width + STATE], b_in[...], b_w[...],
+        block, ext_b, halo[:, width : width + STATE], b_raw[here], b_w[...],
         wide_row(b_b, 2 * group), age,
     )
     x_out[...] = x
@@ -118,12 +136,6 @@
     tail = jnp.where(ahead >= last_start, jnp.exp(last - running), 0.0) * step
     block_start = (first + block * BLOCK).astype(f32)
     carry = jnp.where(last_start < block_start, jnp.exp(last), 0.0)
-
-    @pl.when(block == 0)
-    def _():
-        state[...] = jnp.zeros_like(state)
-        total[...] = jnp.zeros_like(total)
-
     heads = dt_in.shape[0]
     old = state[...]
     states_out[0] = old.astype(bf16)
@@ -170,13 +182,22 @@
 
 def inside_kernel(
     place, x_ref, b_ref, c_in, z_in, halo, dt_in, c_w, c_b, states, dt_bias, a_log, skip, doc_len,
-    c_out, base_out, gain_out, ext_c, total,
+    c_out, base_out, gain_out, ext_c, total, c_raw, arrived,
 ):
     block = pl.program_id(0)
     group, first = place[0], place[1]
+
+    @pl.when(block == 0)
+    def _():
+        columns = pl.ds(pl.multiple_of((GROUPS + group) * STATE, STATE), STATE)
+        copy = pltpu.make_async_copy(c_in.at[:, columns], c_raw, arrived)
+        copy.start()
+        copy.wait()
+
+    here = pl.ds(pl.multiple_of(block * BLOCK, BLOCK), BLOCK)
     start, places = doc_starts(doc_len[...], first + block * BLOCK)
     c = conv_silu(
-        block, ext_c, halo[:, 2 * STATE : 3 * STATE], c_in[...], c_w[...],
+        block, ext_c, halo[:, 2 * STATE : 3 * STATE], c_raw[here], c_w[...],
         wide_row(c_b, 2 * (GROUPS + group)), places - start,
     )
     c_out[...] = c
@@ -226,28 +247,23 @@
         now = factor * now + message[:, :at]
 
 
-def join_kernel(mine, c_ref, base, gain, gated_out, copies, entering, squares):
-    block = pl.program_id(0)
-
-    @pl.when(block == 0)
-    def _():
-        rows = []
-        for piece in range(mine.shape[0]):
-            part = mine[piece].astype(f32)
-            rows += [part[:, :STATE], part[:, STATE:]]
-        entering[...] = jnp.concatenate(rows, axis=0).astype(bf16)
-
-    gated = base[...] + gain[...] * dot_rows(c_ref[...], entering[...])
-    gated_out[...] = gated
-    high, low = split_pair(gated * gated)
-    ones = jnp.ones((8, gated.shape[1]), bf16)
-    sums = dot_rows(ones, high) + dot_rows(ones, low)
-    squares[pl.ds(2 * block, 1), :] = sums[0:1, :128]
-    squares[pl.ds(2 * block + 1, 1), :] = sums[0:1, 128:]
-
-    @pl.when(block == pl.num_programs(0) - 1)
-    def _():
-        copies[...] = jnp.broadcast_to(squares[...].astype(bf16)[None], copies.shape)
+def join_kernel(mine, c_ref, base, gain, gated_out, copies):
+    rows = []
+    for piece in range(mine.shape[0]):
+        part = mine[piece].astype(f32)
+        rows += [part[:, :STATE], part[:, STATE:]]
+    entering = jnp.concatenate(rows, axis=0).astype(bf16)
+    ones = jnp.ones((8, base.shape[1]), bf16)
+    squares = []
+    for block in range(base.shape[0] // BLOCK):
+        here = slice(block * BLOCK, (block + 1) * BLOCK)
+        gated = base[here] + gain[here] * dot_rows(c_ref[here], entering)
+        gated_out[here] = gated
+        high, low = split_pair(gated * gated)
+        sums = dot_rows(ones, high) + dot_rows(ones, low)
+        squares += [sums[0:1, :128], sums[0:1, 128:]]
+    packed = jnp.concatenate(squares, axis=0).astype(bf16)
+    copies[...] = jnp.broadcast_to(packed[None], copies.shape)
 
 
 def finish_kernel(channels, everything, gated, norm, out, scale):
@@ -301,27 +317,27 @@
         return pl.BlockSpec(shape, lambda i, *_: (0,) * len(shape))
 
     tokens = pl.BlockSpec((BLOCK, width), lambda i, *_: (i, 0))
-    b_cols = pl.BlockSpec((BLOCK, STATE), lambda i, s: (i, s[0]))
-    c_cols = pl.BlockSpec((BLOCK, STATE), lambda i, s: (i, s[0] + GROUPS))
+    in_place = pl.BlockSpec(memory_space=pltpu.HBM)
     b_taps = pl.BlockSpec((CONV, STATE), lambda i, s: (0, s[0]))
     c_taps = pl.BlockSpec((CONV, STATE), lambda i, s: (0, s[0] + GROUPS))
     dt_cols = pl.BlockSpec((heads, BLOCK), lambda i, *_: (0, i))
     scalars = pl.BlockSpec(memory_space=pltpu.SMEM)
     block_states = pl.BlockSpec((1, width, STATE), lambda i, *_: (i, 0, 0))
 
-    def call(kernel, prefetch, in_specs, out_specs, out_shape, scratch, grid=(blocks,), cost=5e8):
+    def call(kernel, prefetch, in_specs, out_specs, out_shape, scratch, grant=GRANT):
         return pl.pallas_call(
             kernel,
             grid_spec=pltpu.PrefetchScalarGridSpec(
                 num_scalar_prefetch=prefetch,
-                grid=grid,
+                grid=(blocks,),
                 in_specs=in_specs,
                 out_specs=out_specs,
                 scratch_shapes=scratch,
             ),
             out_shape=out_shape,
+            compiler_params=pltpu.CompilerParams(vmem_limit_bytes=grant),
             cost_estimate=pl.CostEstimate(
-                flops=int(cost), bytes_accessed=4_000_000, transcendentals=1_000_000
+                flops=500_000_000, bytes_accessed=4_000_000, transcendentals=1_000_000
             ),
         )
 
@@ -331,7 +347,7 @@
         ends_kernel,
         1,
         [
-            tokens, b_cols, whole(HALO, width + 2 * STATE), dt_cols, whole(CONV, width),
+            in_place, in_place, whole(HALO, width + 2 * STATE), dt_cols, whole(CONV, width),
             whole(*x_b.shape), b_taps, whole(*bc_b.shape), scalars, scalars, whole(*docs.shape),
         ],
         [tokens, tokens, block_states, whole(shard_count, HALO, message)],
@@ -346,14 +362,18 @@
             pltpu.VMEM((BLOCK + HALO, STATE), f32),
             pltpu.VMEM((width, STATE), f32),
             pltpu.VMEM((8, 1), f32),
-        ],
+            pltpu.VMEM((rows, width), bf16),
+            pltpu.VMEM((rows, STATE), bf16),
+            pltpu.SemaphoreType.DMA((2,)),
+        ],
+        WIDE_GRANT,
     )(place, x_in, bc_in, halo, dt_in, conv_x_w, x_b, conv_bc_w, bc_b, dt_bias, a_log, docs)
     got = lax.all_to_all(sent, "context", split_axis=0, concat_axis=0, tiled=True)
     c, base, gain = call(
         inside_kernel,
         1,
         [
-            tokens, tokens, c_cols, tokens, whole(HALO, width + 2 * STATE), dt_cols, c_taps,
+            tokens, tokens, in_place, tokens, whole(HALO, width + 2 * STATE), dt_cols, c_taps,
             whole(*bc_b.shape), block_states, scalars, scalars, scalars, whole(*docs.shape),
         ],
         [tokens, tokens, tokens],
@@ -362,22 +382,30 @@
             struct((rows, width), f32),
             struct((rows, width), f32),
         ],
-        [pltpu.VMEM((BLOCK + HALO, STATE), f32), pltpu.VMEM((1, 8), f32)],
+        [
+            pltpu.VMEM((BLOCK + HALO, STATE), f32),
+            pltpu.VMEM((1, 8), f32),
+            pltpu.VMEM((rows, STATE), bf16),
+            pltpu.SemaphoreType.DMA,
+        ],
+        WIDE_GRANT,
     )(
         place, x, b, bc_in, z_in, halo, dt_in, conv_bc_w, bc_b, states, dt_bias, a_log,
         skip_gain, docs,
     )
     back = pl.pallas_call(
-        scan_kernel, out_shape=struct((shard_count, HALO, 2 * STATE), bf16)
+        scan_kernel,
+        out_shape=struct((shard_count, HALO, 2 * STATE), bf16),
+        compiler_params=pltpu.CompilerParams(vmem_limit_bytes=GRANT),
     )(got)
     mine = lax.all_to_all(back, "context", split_axis=0, concat_axis=0, tiled=True)
-    gated, copies = call(
+    gated, copies = pl.pallas_call(
         join_kernel,
-        0,
-        [whole(shard_count, HALO, 2 * STATE), tokens, tokens, tokens],
-        [tokens, whole(head_count, rows // 128, 128)],
-        [struct((rows, width), f32), struct((head_count, rows // 128, 128), bf16)],
-        [pltpu.VMEM((width, STATE), bf16), pltpu.VMEM((rows // 128, 128), f32)],
+        out_shape=[
+            struct((rows, width), f32),
+            struct((head_count, rows // 128, 128), bf16),
+        ],
+        compiler_params=pltpu.CompilerParams(vmem_limit_bytes=GRANT),
     )(mine, c, base, gain)
     everything = lax.all_to_all(copies, "head", split_axis=0, concat_axis=0, tiled=True)
     return call(

time: 103 us -> 104 us (level)
  local copies, waits for them, and re-layouts: 2.78 us -> 13.8 us
  Pallas kernels: 27.9 us -> 20.3 us
  waiting for transfers between devices: 2.69 us -> 0.8 us
    unnamed x4 -> x48, local copies, waits for them, and re-layouts: 1.25 us -> 12.2 us
    pallas_call x3, Pallas kernels: 22.5 us -> 17.5 us  [the longest x1 8.93 us: shards(): call(inside_kernel, 1, [tokens, tokens, in_place, tokens, whole(HALO, wid...]
    all_to_all x1, waiting for transfers between devices: 2.49 us -> 0.07 us  [shards(): lax.all_to_all(back, 'context', split_axis=0, concat_axis=0, tiled=True)]
    pallas_call x1, Pallas kernels: 3.78 us -> 2.06 us  [shards(): call(functools.partial(finish_kernel, float(heads_total * HEAD_DIM)), 0,...]
  transfers between devices with their start and end apart: 2 -> 2, of which waited for: 2 -> 2; matrix products, arithmetic and copies ran while one was open for 1% -> 0% of each run, Pallas kernels for 9% -> 9%
where the time goes in v3:
time: 104 us; the launch traced here: 103 us
  blocking collectives  56.6 us (54%)
  Pallas kernels  20.3 us (20%)
  local copies, waits for them, and re-layouts  13.8 us (13%)
  starting transfers between devices  11.3 us (11%)
    all_to_all x1, blocking collectives, shards(): lax.all_to_all(sent, 'context', split_axis=0, concat_axis=0, tiled=True)  31.4 us
    all_to_all x1, blocking collectives, shards(): lax.all_to_all(copies, 'head', split_axis=0, concat_axis=0, tiled=True)  25.2 us
    unnamed x48, local copies, waits for them, and re-layouts  12.2 us
    pallas_call x1, Pallas kernels, shards(): call(inside_kernel, 1, [tokens, tokens, in_place, tokens, whole(HALO, wid...  8.93 us
    pallas_call x1, Pallas kernels, shards(): call(ends_kernel, 1, [in_place, in_place, whole(HALO, width + 2 * STATE),...  7.65 us
    all_to_all x1, starting transfers between devices, shards(): lax.all_to_all(back, 'context', split_axis=0, concat_axis=0, tiled=True)  6.47 us
    ppermute x1, starting transfers between devices, shards(): halo = lax.ppermute(last, 'context', pairs)  4.81 us
  transfers between devices with their start and end apart: 2, of which 2 were waited for; matrix products, arithmetic and copies ran while one was open for 0% of the time, Pallas kernels for 9%

profile of v3, /device:TPU:1, one launch (start us, length us, event | category | flops | bytes accessed | tf_op | source)
XLA Modules:
  0.0 103.1 jit_solution(17731477552039188542)
XLA Ops:
  0.1 0.7 slice.6
  0.8 0.8 slice.7
  1.7 4.8 %collective-permute-start = (bf16[8,768]{1,0:T(8,128)(2,1)S(1)}, bf16[8,768]{1,0:T(8,128)(2,1)S(1)}, u32[]{:S(2)}, u32[]{:S(2)}) collective-permute-start(bf16[8,768]{1,0:T(8,128)(2,1)S(1)} %pad_maximum_fusion), channel_id=1, source_target_pairs={{0,64},{64,128},{128,192},{192,256},{256,320},{320,384},{384,448},... | collective-permute-start | bytes 36872 | tf_op jit(solution)/shard_map/ppermute | solution.py:310
  6.6 0.7 collective-permute-done.halo
  7.3 1.0 %copy-done = bf16[1024,256]{1,0:T(8,128)(2,1)S(1)} copy-done((bf16[1024,256]{1,0:T(8,128)(2,1)S(1)}, bf16[1024,256]{1,0:T(8,128)(2,1)}, u32[]{:S(2)}) %copy-start) | copy-done | bytes 524312
  8.3 0.8 copy-done.8
  9.2 0.7 copy-done.10
  9.9 0.7 copy-done.12
  10.6 0.7 copy-done.14
  13.3 0.7 copy-done.21
  13.9 7.6 %shard_map.127 = (bf16[1024,256]{1,0:T(8,128)(2,1)S(1)}, bf16[1024,256]{1,0:T(8,128)(2,1)S(1)}, bf16[4,256,256]{2,1,0:T(8,128)(2,1)S(1)}, bf16[16,8,640]{2,1,0:T(8,128)(2,1)S(1)}) custom-call(s32[2]{0:T(128)S(1)} %pad_add_fusion.place, bf16[1024,256]{1,0:T(8,128)(2,1)S(1)} %copy-done, bf16[1024,4096]{1,0:T(8,128)(2,1)} %c_in.1, ...), custom_call_target="tpu_custom_call" | custom-call | flops 500000000 | bytes 4000000 | tf_op jit(solution)/shard_map/pallas_call | solution.py:346
  21.6 0.8 copy-done.2
  22.4 0.8 copy-done.4
  23.2 31.4 %all_to_all.15.got = bf16[16,8,640]{2,1,0:T(8,128)(2,1)S(1)} all-to-all(bf16[16,8,640]{2,1,0:T(8,128)(2,1)S(1)} %get-tuple-element.14), channel_id=1, replica_groups=mesh['context'=16,'head'=64] {'context'}, dimensions={0} | all-to-all | bytes 327680 | tf_op jit(solution)/shard_map/all_to_all | solution.py:371
  54.6 0.8 shard_map.128
  55.4 6.5 %all-to-all-start.1 = ((bf16[16,8,512]{2,1,0:T(8,128)(2,1)}), bf16[16,8,512]{2,1,0:T(8,128)(2,1)S(1)}, u32[]{:S(2)}, u32[]{:S(2)}) async-start(bf16[16,8,512]{2,1,0:T(8,128)(2,1)} %shard_map.128), calls=%async_computation.1 | async-start | bytes 262144 | tf_op jit(solution)/shard_map/all_to_all | solution.py:401
  62.0 1.0 %copy-done.3 = bf16[1024,256]{1,0:T(8,128)(2,1)S(1)} copy-done((bf16[1024,256]{1,0:T(8,128)(2,1)S(1)}, bf16[1024,256]{1,0:T(8,128)(2,1)}, u32[]{:S(2)}) %copy-start.3) | copy-done | bytes 524312
  63.0 1.0 %copy-done.5 = bf16[4,256,256]{2,1,0:T(8,128)(2,1)S(1)} copy-done((bf16[4,256,256]{2,1,0:T(8,128)(2,1)S(1)}, bf16[4,256,256]{2,1,0:T(8,128)(2,1)}, u32[]{:S(2)}) %copy-start.5) | copy-done | bytes 524312
  64.1 8.9 %shard_map.129 = (bf16[1024,256]{1,0:T(8,128)(2,1)S(1)}, f32[1024,256]{1,0:T(8,128)S(1)}, f32[1024,256]{1,0:T(8,128)S(1)}) custom-call(s32[2]{0:T(128)S(1)} %pad_add_fusion.place, bf16[1024,256]{1,0:T(8,128)(2,1)S(1)} %get-tuple-element.15.x_ref, bf16[1024,256]{1,0:T(8,128)(2,1)S(1)} %copy-done.3, bf16[1024,4096]{1,0:T(8,128)(2,1)} %c_in.1, ...), custom_call_target="tpu_custom_call" | custom-call | flops 500000000 | bytes 4000000 | tf_op jit(solution)/shard_map/pallas_call | solution.py:372
  73.0 0.8 copy-done.6
  73.9 1.0 %copy-done.7 = bf16[1024,256]{1,0:T(8,128)(2,1)S(1)} copy-done((bf16[1024,256]{1,0:T(8,128)(2,1)S(1)}, bf16[1024,256]{1,0:T(8,128)(2,1)}, u32[]{:S(2)}) %copy-start.7) | copy-done | bytes 524312
  74.9 0.9 shard_map.130
  75.8 25.2 %all_to_all.16.everything = bf16[64,8,128]{2,1,0:T(8,128)(2,1)S(1)} all-to-all(bf16[64,8,128]{2,1,0:T(8,128)(2,1)S(1)} %get-tuple-element.21), channel_id=1, replica_groups=mesh['context'=16,'head'=64] {'head'}, dimensions={0} | all-to-all | bytes 262144 | tf_op jit(solution)/shard_map/all_to_all | solution.py:410
  101.0 2.1 %shard_map.131 = bf16[1024,256]{1,0:T(8,128)(2,1)} custom-call(bf16[64,8,128]{2,1,0:T(8,128)(2,1)S(1)} %all_to_all.16.everything, f32[1024,256]{1,0:T(8,128)S(1)} %get-tuple-element.22.gated, f32[2,128]{1,0:T(2,128)S(1)} %bitcast.11), custom_call_target="tpu_custom_call" | custom-call | flops 500000000 | bytes 4000000 | tf_op jit(solution)/shard_map/pallas_call | solution.py:411
  (40 shorter events, 2.2 us)
Async XLA Ops:
  0.0 61.9 %copy-start.18 = (f32[4]{0:T(128)S(1)}, f32[4]{0:T(128)}, u32[]{:S(2)}) copy-start(f32[4]{0:T(128)} %a_log.3) | copy-start | bytes 52
  0.0 61.9 %copy-start.16 = (f32[4]{0:T(128)S(1)}, f32[4]{0:T(128)}, u32[]{:S(2)}) copy-start(f32[4]{0:T(128)} %dt_bias.3) | copy-start | bytes 52
  0.0 61.9 %copy-start.9 = (f32[4,4096]{1,0:T(4,128)S(1)}, f32[4,4096]{1,0:T(4,128)}, u32[]{:S(2)}) copy-start(f32[4,4096]{1,0:T(4,128)} %c_w.1) | copy-start | bytes 196612
  0.0 61.9 %copy-start.13 = (bf16[4,1024]{1,0:T(4,128)(2,1)S(1)}, bf16[4,1024]{1,0:T(4,128)(2,1)}, u32[]{:S(2)}) copy-start(bf16[4,1024]{1,0:T(4,128)(2,1)} %dt_in.3) | copy-start | bytes 24580
  0.0 61.9 %copy-start.20 = (s32[64]{0:T(128)S(1)}, s32[64]{0:T(128)}, u32[]{:S(2)}) copy-start(s32[64]{0:T(128)} %param.25) | copy-start | bytes 772
  0.0 61.9 %copy-start.11 = (f32[4096]{0:T(1024)S(1)}, f32[4096]{0:T(1024)}, u32[]{:S(2)}) copy-start(f32[4096]{0:T(1024)} %param.20) | copy-start | bytes 49156
  0.0 61.9 %copy-start.22 = (f32[4]{0:T(128)S(1)}, f32[4]{0:T(128)}, u32[]{:S(2)}) copy-start(f32[4]{0:T(128)} %skip.1) | copy-start | bytes 52
  1.7 5.6 %collective-permute-start = (bf16[8,768]{1,0:T(8,128)(2,1)S(1)}, bf16[8,768]{1,0:T(8,128)(2,1)S(1)}, u32[]{:S(2)}, u32[]{:S(2)}) collective-permute-start(bf16[8,768]{1,0:T(8,128)(2,1)S(1)} %pad_maximum_fusion), channel_id=1, source_target_pairs={{0,64},{64,128},{128,192},{192,256},{256,320},{320,384},{384,448},... | collective-permute-start | bytes 36872 | tf_op jit(solution)/shard_map/ppermute | solution.py:310
  7.3 1.0 %copy-start = (bf16[1024,256]{1,0:T(8,128)(2,1)S(1)}, bf16[1024,256]{1,0:T(8,128)(2,1)}, u32[]{:S(2)}) copy-start(bf16[1024,256]{1,0:T(8,128)(2,1)} %x_in.1) | copy-start | bytes 1572868
  8.3 0.8 copy-start.8
  9.2 0.7 copy-start.10
  9.9 0.7 copy-start.12
  10.6 0.7 copy-start.14
  11.3 0.7 copy-start.15
  13.3 0.7 copy-start.21
  13.9 48.1 %copy-start.1 = (bf16[1024,256]{1,0:T(8,128)(2,1)S(1)}, bf16[1024,256]{1,0:T(8,128)(2,1)}, u32[]{:S(2)}) copy-start(bf16[1024,256]{1,0:T(8,128)(2,1)} %z_in.1) | copy-start | bytes 1572868
  21.6 0.8 copy-start.2
  22.4 0.8 copy-start.4
  23.2 77.8 %copy-start.23 = (f32[256]{0:T(256)S(1)}, f32[256]{0:T(256)}, u32[]{:S(2)}) copy-start(f32[256]{0:T(256)} %param.24) | copy-start | bytes 3076
  55.4 18.5 %all-to-all-start.1 = ((bf16[16,8,512]{2,1,0:T(8,128)(2,1)}), bf16[16,8,512]{2,1,0:T(8,128)(2,1)S(1)}, u32[]{:S(2)}, u32[]{:S(2)}) async-start(bf16[16,8,512]{2,1,0:T(8,128)(2,1)} %shard_map.128), calls=%async_computation.1 | async-start | bytes 262144 | tf_op jit(solution)/shard_map/all_to_all | solution.py:401
  62.0 1.0 %copy-start.3 = (bf16[1024,256]{1,0:T(8,128)(2,1)S(1)}, bf16[1024,256]{1,0:T(8,128)(2,1)}, u32[]{:S(2)}) copy-start(bf16[1024,256]{1,0:T(8,128)(2,1)} %copy-done.2) | copy-start | bytes 1572868
  63.0 1.0 %copy-start.5 = (bf16[4,256,256]{2,1,0:T(8,128)(2,1)S(1)}, bf16[4,256,256]{2,1,0:T(8,128)(2,1)}, u32[]{:S(2)}) copy-start(bf16[4,256,256]{2,1,0:T(8,128)(2,1)} %copy-done.4) | copy-start | bytes 1572868
  73.0 0.8 copy-start.6
  73.9 1.0 %copy-start.7 = (bf16[1024,256]{1,0:T(8,128)(2,1)S(1)}, bf16[1024,256]{1,0:T(8,128)(2,1)}, u32[]{:S(2)}) copy-start(bf16[1024,256]{1,0:T(8,128)(2,1)} %copy-done.6) | copy-start | bytes 1572868
  (2 other events, 1.3 us)
